TPU v7x, 32 devices: a whole 2x2x4 slice. The times are simulated.
32 devices in a mesh: grp: 2 (over x), seq: 16 (over z, y, core).
Axes of the slice: x: 2, y: 2, z: 4, core: 2. Of those that a mesh axis runs over, the one named last changes fastest.
Arguments:
- tokens: bfloat16 [4, 3072, 768], P('grp', 'seq'), may hold values from -6 to 6
- valid_len: int32 [4], P('grp'), may hold values from 768 to 3072, as said below
- query_weight: bfloat16 [768, 768], P(('grp', 'seq')), may hold values from -0.21875 to 0.21875
- query_bias: bfloat16 [768], P(('grp', 'seq')), may hold values from -3 to 3
- key_weight: bfloat16 [768, 768], P(('grp', 'seq')), may hold values from -0.21875 to 0.21875
- value_weight: bfloat16 [768, 768], P(('grp', 'seq')), may hold values from -0.21875 to 0.21875
- value_bias: bfloat16 [768], P(('grp', 'seq')), may hold values from -3 to 3
- output_weight: bfloat16 [768, 768], P(('grp', 'seq')), may hold values from -6 to 6
- output_bias: bfloat16 [768], P(('grp', 'seq')), may hold values from -3 to 3
- first_gain: bfloat16 [768], P(('grp', 'seq')), may hold values from 0.099609375 to 1.8984375
- first_shift: bfloat16 [768], P(('grp', 'seq')), may hold values from -3 to 3
- inner_weight: bfloat16 [768, 3072], P(('grp', 'seq')), may hold values from -0.21875 to 0.21875
- inner_bias: bfloat16 [3072], P(('grp', 'seq')), may hold values from -3 to 3
- outer_weight: bfloat16 [3072, 768], P(('grp', 'seq')), may hold values from -0.109375 to 0.109375
- outer_bias: bfloat16 [768], P(('grp', 'seq')), may hold values from -3 to 3
- second_gain: bfloat16 [768], P(('grp', 'seq')), may hold values from 0.099609375 to 1.8984375
- second_shift: bfloat16 [768], P(('grp', 'seq')), may hold values from -3 to 3
- grad_out: bfloat16 [4, 3072, 768], P('grp', 'seq'), may hold values from -6 to 6
Outputs:
- layer_output: bfloat16 [4, 3072, 768], P('grp', 'seq')
- dtokens: bfloat16 [4, 3072, 768], P('grp', 'seq')
- dquery_weight: float32 [768, 768], P('seq')
- dquery_bias: float32 [768], P('seq')
- dkey_weight: float32 [768, 768], P('seq')
- dvalue_weight: float32 [768, 768], P('seq')
- dvalue_bias: float32 [768], P('seq')
- doutput_weight: float32 [768, 768], P('seq')
- doutput_bias: float32 [768], P('seq')
- dfirst_gain: float32 [768], P('seq')
- dfirst_shift: float32 [768], P('seq')
- dinner_weight: float32 [768, 3072], P('seq')
- dinner_bias: float32 [3072], P('seq')
- douter_weight: float32 [3072, 768], P('seq')
- douter_bias: float32 [768], P('seq')
- dsecond_gain: float32 [768], P('seq')
- dsecond_shift: float32 [768], P('seq')
Inputs may be any that keep to these rules, and one draw needn't show every extreme that they name: Sequence n takes only its first valid_len[n] positions as keys; in every draw some sequence takes all 3072.
All inputs are finite; a program needn't handle non-finite values.
Results may differ from a plain program's by a relative error of at most 0.023.
Values may be sent and summed in bfloat16 or wider, within the bound.
No kernel may reach another device: no remote copies, remote signals or barrier semaphores. Data moves between devices by JAX's collectives and lax.ppermute only.
A program may use at most 320 MiB of HBM per device.

v0:
```python
from functools import partial

import jax
import jax.numpy as jnp
from jax import lax
from jax.experimental import pallas as pl
from jax.experimental.pallas import tpu as pltpu
from jax.sharding import PartitionSpec as P

HEADS = 12
HEAD = 64
HEAD_GROUPS = 4
GROUP_WIDTH = HEADS * HEAD // HEAD_GROUPS
NH = HEADS // HEAD_GROUPS
BF16 = jnp.bfloat16
F32 = jnp.float32

score_scale = 0.125
epsilon = 1e-12
masked_score = -1e30


def log2_of(size):
    return size.bit_length() - 1


def flip(value, axis, size, mask):
    return lax.ppermute(value, axis, [(i, i ^ mask) for i in range(size)])


def in_order(mine, theirs, bit):
    return jnp.where(bit == 0, jnp.stack([mine, theirs]), jnp.stack([theirs, mine]))


def pick(pair, bit):
    return jnp.where(bit == 0, pair[0], pair[1])


def layer_norm(hidden, norm_gain, norm_shift):
    centred = hidden - jnp.mean(hidden, axis=-1, keepdims=True)
    spread = jnp.mean(centred * centred, axis=-1, keepdims=True)
    return centred * lax.rsqrt(spread + epsilon) * norm_gain + norm_shift


def dot(left, right):
    return jnp.dot(left, right, preferred_element_type=jnp.float32)


def dot_t(left, right):
    return lax.dot_general(left, right, (((1,), (1,)), ((), ())), preferred_element_type=jnp.float32)


def t_dot(left, right):
    return lax.dot_general(left, right, (((0,), (0,)), ((), ())), preferred_element_type=jnp.float32)


def column_sums(matrix):
    return jnp.sum(matrix.astype(jnp.float32), axis=0)


def thirds(x):
    hi=x.astype(BF16)
    r=x-hi.astype(F32)
    mid=r.astype(BF16)
    lo=(r-mid.astype(F32)).astype(BF16)
    return hi,mid,lo

def fwd_body(q_ref, kv_ref, kb_ref, c_ref, cf_ref, st_ref, kt, va, oacc, lacc, *, bq):
    i=pl.program_id(0); h=pl.program_id(1)
    W=NH*HEAD
    @pl.when((i==0)&(h==0))
    def _():
        tail=kb_ref[:,HEAD:]
        for g in range(NH):
            ka=jnp.concatenate([kv_ref[:,g*HEAD:(g+1)*HEAD],tail],axis=1)
            kt[g]=ka.T
            va[g]=jnp.concatenate([kv_ref[:,W+g*HEAD:W+(g+1)*HEAD],tail],axis=1)
    one=jnp.where(lax.broadcasted_iota(jnp.int32,(bq,HEAD),1)==0,1.0,0.0).astype(BF16)
    def head(g):
        qa=jnp.concatenate([q_ref[:,g*HEAD:(g+1)*HEAD],one],axis=1)
        s=dot(qa,kt[g])
        m=jnp.max(s,axis=1,keepdims=True)
        p=jnp.exp(s-m).astype(BF16)
        o=dot(p,va[g])
        l=o[:,HEAD+1:HEAD+2]
        oacc[g]=o/l
        lacc[g]=jnp.broadcast_to(m+jnp.log(l),(bq,128))
    for g in range(NH):
        @pl.when(h==g)
        def _(): head(g)
    @pl.when(h==NH-1)
    def _():
        c=jnp.concatenate([oacc[g][:,:HEAD] for g in range(NH)],axis=1)
        c_ref[...]=c.astype(BF16)
        cf_ref[...]=c
        lane=lax.broadcasted_iota(jnp.int32,(bq,128),1)
        st=lacc[0]
        for g in range(1,NH): st=jnp.where(lane==g,lacc[g],st)
        st_ref[...]=st

def attend_forward(q,kv,kb,bq=256):
    n,W=q.shape; L=kv.shape[0]
    return pl.pallas_call(partial(fwd_body,bq=bq),
        grid=(n//bq,NH),
        in_specs=[pl.BlockSpec((bq,W),lambda i,h:(i,0)),pl.BlockSpec((L,2*W),lambda i,h:(0,0)),pl.BlockSpec((L,128),lambda i,h:(0,0))],
        out_specs=[pl.BlockSpec((bq,W),lambda i,h:(i,0)),pl.BlockSpec((bq,W),lambda i,h:(i,0)),pl.BlockSpec((bq,128),lambda i,h:(i,0))],
        out_shape=[jax.ShapeDtypeStruct((n,W),BF16),jax.ShapeDtypeStruct((n,W),F32),jax.ShapeDtypeStruct((n,128),F32)],
        scratch_shapes=[pltpu.VMEM((NH,128,L),BF16),pltpu.VMEM((NH,L,128),BF16),pltpu.VMEM((NH,bq,128),F32),pltpu.VMEM((NH,bq,128),F32)],
        cost_estimate=pl.CostEstimate(flops=16*n*L*W, transcendentals=NH*n*L, bytes_accessed=4*n*L),
        name="attend_forward",
    )(q,kv,kb)

def bwd_body(bit_ref, q_ref, kv_ref, kb_ref, cf_ref, st_ref, dc_ref, dq_ref, sent_ref, kept_ref, qt, qn, dct, dcn, dqt, dk, dv, *, nk):
    j=pl.program_id(0); h=pl.program_id(1)
    W=NH*HEAD
    n=q_ref.shape[0]
    @pl.when((j==0)&(h==0))
    def _():
        pad=jnp.zeros((n,256-W),BF16)
        row=lax.broadcasted_iota(jnp.int32,(16,n),0)
        lane=lax.broadcasted_iota(jnp.int32,(8,W),1)
        head_row=lax.broadcasted_iota(jnp.int32,(8,W),0)
        pick=jnp.where((lane>=head_row*HEAD)&(lane<head_row*HEAD+HEAD),1.0,0.0).astype(BF16)
        prod=dc_ref[...].astype(F32)*cf_ref[...]
        hi,mid,lo=thirds(prod)
        deltas=dot_t(pick,hi)+dot_t(pick,mid)+dot_t(pick,lo)
        stats=st_ref[...].T
        q_t=jnp.concatenate([q_ref[...],pad],axis=1).T
        d_t=jnp.concatenate([dc_ref[...],pad],axis=1).T
        def tail(x,first):
            hi,mid,lo=(v.astype(F32) for v in thirds(-x))
            z=jnp.where(row==1,hi,jnp.where(row==2,mid,jnp.where(row==3,lo,0.0)))
            return jnp.where(row==0,first,z).astype(BF16)
        rest=jnp.zeros((HEAD-16,n),BF16)
        for g in range(NH):
            cols=slice(g*HEAD,(g+1)*HEAD)
            for t,x,first,dst in ((q_t,stats,1.0,qt),(d_t,deltas,0.0,dct)):
                dst[g,:HEAD]=t[cols]
                dst[g,HEAD:HEAD+16]=tail(x[g:g+1],first)
                dst[g,HEAD+16:]=rest
            qn[g]=q_ref[:,cols]
            dcn[g]=dc_ref[:,cols]
        dqt[...]=jnp.zeros_like(dqt)
    key_tail=kb_ref[:,HEAD:]
    def head(g):
        k=kv_ref[:,g*HEAD:(g+1)*HEAD]
        ka=jnp.concatenate([k,key_tail],axis=1)
        va=jnp.concatenate([kv_ref[:,W+g*HEAD:W+(g+1)*HEAD],key_tail],axis=1)
        p=jnp.exp(dot(ka,qt[g]))
        dp=dot(va,dct[g])
        ds=(p*dp).astype(BF16)
        dv[g]=dot(p.astype(BF16),dcn[g])
        dk[g]=dot(ds,qn[g])
        dqt[g]=dqt[g]+t_dot(ka,ds)[:HEAD]
    for g in range(NH):
        @pl.when(h==g)
        def _(): head(g)
    @pl.when(h==NH-1)
    def _():
        dkv=jnp.concatenate([dk[g] for g in range(NH)]+[dv[g] for g in range(NH)],axis=1)
        @pl.when(j<nk//2)
        def _():
            sent_ref[...]=dkv.astype(BF16)
        @pl.when(j>=nk//2)
        def _():
            kept_ref[...]=dkv
    @pl.when((h==NH-1)&(j==nk-1))
    def _():
        for g in range(NH):
            dq_ref[:,g*HEAD:(g+1)*HEAD]=(dqt[g].T*0.125).astype(BF16)

def attend_backward(q,kv,kb,cf,st,dc,bit,bk=768):
    n,W=q.shape; L=kv.shape[0]; nk=L//bk; half=nk//2
    full=lambda a: pl.BlockSpec(a.shape,lambda j,h,b:(0,0))
    key=lambda j,h,b:(jnp.where(j<half,(1-b[0])*half+j,b[0]*half+j-half),0)
    return pl.pallas_call(partial(bwd_body,nk=nk),
        grid_spec=pltpu.PrefetchScalarGridSpec(
            num_scalar_prefetch=1,
            grid=(nk,NH),
            in_specs=[full(q),pl.BlockSpec((bk,2*W),key),pl.BlockSpec((bk,128),key),full(cf),full(st),full(dc)],
            out_specs=[pl.BlockSpec((n,W),lambda j,h,b:(0,0)),
                pl.BlockSpec((bk,2*W),lambda j,h,b:(jnp.minimum(j,half-1),0)),
                pl.BlockSpec((bk,2*W),lambda j,h,b:(jnp.maximum(j-half,0),0))],
            scratch_shapes=[pltpu.VMEM((NH,2*HEAD,n),BF16),pltpu.VMEM((NH,n,HEAD),BF16),pltpu.VMEM((NH,2*HEAD,n),BF16),pltpu.VMEM((NH,n,HEAD),BF16),
                pltpu.VMEM((NH,HEAD,n),F32),pltpu.VMEM((NH,bk,HEAD),F32),pltpu.VMEM((NH,bk,HEAD),F32)]),
        out_shape=[jax.ShapeDtypeStruct((n,W),BF16),jax.ShapeDtypeStruct((L//2,2*W),BF16),jax.ShapeDtypeStruct((L//2,2*W),F32)],
        name="attend_backward",
    )(bit,q,kv,kb,cf,st,dc)


def feed_grads_body(y_ref, dz_ref, a_ref, do_ref, out_ref, *, chips):
    width = y_ref.shape[1]
    r_in, r_out = width // chips, a_ref.shape[1] // chips
    half = chips // 2
    for j in range(2):
        grad = t_dot(y_ref[...], dz_ref[:, j * width : (j + 1) * width]).astype(BF16)
        for q in range(chips):
            out_ref[q, j * r_in : (j + 1) * r_in] = grad[q * r_in : (q + 1) * r_in]
        grad = t_dot(a_ref[:, j * width : (j + 1) * width], do_ref[...]).astype(BF16)
        for q in range(half):
            out_ref[j * half + q, 2 * r_in :] = grad[q * r_out : (q + 1) * r_out]


def feed_grads(y, dz, a, do, chips):
    width = y.shape[1]
    return pl.pallas_call(
        partial(feed_grads_body, chips=chips),
        out_shape=jax.ShapeDtypeStruct((chips, (2 * width + a.shape[1]) // chips, width), BF16),
        cost_estimate=pl.CostEstimate(
            flops=4 * width * y.shape[0] * dz.shape[1], transcendentals=0, bytes_accessed=10 * width * width * 2
        ),
        name="feed_grads",
    )(y, dz, a, do)


def other_grads_body(dz_ref, ctx_ref, da_ref, do_ref, vec_ref, out_ref, *, chips):
    width = da_ref.shape[1]
    r_ctx = ctx_ref.shape[1] // chips
    grad = t_dot(ctx_ref[...], da_ref[...]).astype(BF16)
    n = do_ref.shape[0]
    ones = jnp.ones((16, da_ref.shape[0]), BF16)
    sums = [dot(ones[:, :n], da_ref[:n])[:1], dot(ones[:, :n], do_ref[...])[:1]]
    sums += [dot(ones, dz_ref[:, j * width : (j + 1) * width])[:1] for j in range(2)]
    small = jnp.concatenate([vec_ref[...]] + sums, axis=0).astype(BF16)
    for q in range(chips):
        out_ref[q, :r_ctx] = grad[q * r_ctx : (q + 1) * r_ctx]
        out_ref[q, r_ctx:] = small


def other_grads(dz, ctx, da, do, vec, chips):
    width = da.shape[1]
    return pl.pallas_call(
        partial(other_grads_body, chips=chips),
        out_shape=jax.ShapeDtypeStruct((chips, ctx.shape[1] // chips + vec.shape[0] + 4, width), BF16),
        cost_estimate=pl.CostEstimate(
            flops=2 * width * ctx.shape[0] * ctx.shape[1], transcendentals=0, bytes_accessed=5 * width * width * 2
        ),
        name="other_grads",
    )(dz, ctx, da, do, vec)


def per_device(
    seq_size,
    grp_size,
    tokens,
    valid_len,
    query_weight,
    query_bias,
    key_weight,
    value_weight,
    value_bias,
    output_weight,
    output_bias,
    first_gain,
    first_shift,
    inner_weight,
    inner_bias,
    outer_weight,
    outer_bias,
    second_gain,
    second_shift,
    grad_out,
):
    bf16 = jnp.bfloat16
    rows, width = tokens.shape[1:]
    feed = inner_weight.shape[1]
    shard = query_weight.shape[0]
    HI, ZO, YO = seq_size // 2, seq_size // 4, 2
    extra_bits = [1 << b for b in range(2, log2_of(ZO))]
    part_bits = [1] + extra_bits
    me = lax.axis_index("seq")
    grp = lax.axis_index("grp")
    z1 = me // HI
    z0 = (me // ZO) % 2
    y0 = (me // YO) % 2
    head_group = 2 * z0 + y0
    my_part = me % 2 + 2 * ((me // 4) % max(ZO // 4, 1))
    n_parts = seq_size // 8

    def sflip(value, mask):
        return flip(value, "seq", seq_size, mask)

    chips = seq_size // 2
    x_mine = pick(tokens, z1)
    x_sent = pick(tokens, 1 - z1)
    half_width = width // 2
    x_theirs = sflip(x_sent, HI)
    x_pair = in_order(x_mine, x_theirs, z1)
    xa, xb = x_pair[:, :, :half_width], x_pair[:, :, half_width:]
    ra, rb = sflip(xa, YO), sflip(xb, ZO)
    xa, xb = in_order(xa, ra, y0), in_order(xb, rb, z0)
    ra, rb = sflip(xa, ZO), sflip(xb, YO)
    xa, xb = in_order(xa, ra, z0), in_order(xb, rb, y0)
    x_all = jnp.concatenate([xa.transpose(2, 0, 1, 3, 4), xb.transpose(2, 1, 0, 3, 4)], axis=-1)
    x_all = x_all.reshape(8 * rows, width)

    core = me % 2
    chips = seq_size // 2
    piece = feed // seq_size
    n_dev = grp_size * seq_size
    half_feed = feed // 2
    split = inner_weight.reshape(shard, chips, 2, piece)
    split = [split[:, :, i].reshape(shard, 2, width).transpose(1, 0, 2).reshape(2 * shard, width) for i in range(2)]
    near = jnp.concatenate([pick(split, 1 - core), output_weight], axis=0)
    far = sflip(near, 1)
    outer_far = lax.ppermute(
        outer_weight,
        ("grp", "seq"),
        [(d, d ^ (1 | grp_size) if d % 2 != (d // grp_size) % 2 else d) for d in range(n_dev)],
    )
    inner_pair = in_order(pick(split, core).reshape(2, shard, width), far[: 2 * shard].reshape(2, shard, width), core)
    packed = jnp.concatenate(
        [
            inner_pair.transpose(1, 0, 2, 3).reshape(4 * shard, width),
            in_order(output_weight, far[2 * shard :], core).reshape(2 * shard, width),
            outer_far,
        ],
        axis=0,
    )
    chip_groups = [[2 * q + i for q in range(chips)] for i in range(2)]
    gathered = lax.all_gather(packed, "seq", axis=0, tiled=False, axis_index_groups=chip_groups)
    first_end = 6 * shard
    gathered = [gathered]
    for b in range(log2_of(grp_size)):
        gathered += [flip(part, "grp", grp_size, 1 << b) for part in gathered]

    def gathered_rows(start, stop):
        parts = [x[:, start:stop] for x in gathered]
        stacks = {i: x[None] for i, x in enumerate(parts)}
        for b in range(log2_of(grp_size)):
            bit = (grp >> b) % 2
            merged = {}
            for i in range(len(stacks) // 2):
                low, high = stacks[2 * i], stacks[2 * i + 1]
                merged[i] = jnp.where(bit == 0, jnp.concatenate([low, high]), jnp.concatenate([high, low]))
            stacks = merged
        return stacks[0].reshape((-1,) + parts[0].shape[1:])

    smalls = jnp.concatenate(
        [query_bias, value_bias, output_bias, first_gain, first_shift, outer_bias, second_gain, second_shift, inner_bias]
    )
    small_rows = 32 - shard if shard == 24 else 8
    grouped = jnp.stack([query_weight, key_weight, value_weight]).reshape(3, shard, HEAD_GROUPS, GROUP_WIDTH)
    grouped = grouped.transpose(2, 1, 0, 3).reshape(HEAD_GROUPS, shard, 3 * GROUP_WIDTH)
    small_block = jnp.zeros((small_rows * 3 * GROUP_WIDTH,), bf16).at[: smalls.shape[0]].set(smalls)
    small_block = jnp.broadcast_to(small_block.reshape(1, small_rows, -1), (HEAD_GROUPS, small_rows, 3 * GROUP_WIDTH))
    grouped = jnp.concatenate([grouped, small_block], axis=1)
    grouped, _ = lax.optimization_barrier((grouped, x_theirs))

    def group_block(k):
        return lax.dynamic_index_in_dim(grouped, head_group ^ k, 0, keepdims=False)

    w0 = group_block(0)
    w1 = sflip(group_block(1), YO)
    w2 = sflip(group_block(2), ZO)
    w3 = sflip(group_block(3), ZO | YO)
    w_all = in_order(in_order(w0, w1, y0), in_order(w2, w3, y0), z0)
    w_all = in_order(w_all, sflip(w_all, HI), z1)
    names = ["z1", "z0", "y0"]
    for b in extra_bits:
        w_all = in_order(w_all, sflip(w_all, b), (me // b) % 2)
        names = ["e%d" % b] + names
    for b in range(log2_of(grp_size)):
        w_all = in_order(w_all, flip(w_all, "grp", grp_size, 1 << b), (grp >> b) % 2)
        names = ["g%d" % b] + names
    w_all = in_order(w_all, sflip(w_all, 1), me % 2)
    names = ["c"] + names
    wanted = ["g%d" % b for b in reversed(range(log2_of(grp_size)))] + ["z1", "z0"]
    wanted += ["e%d" % b for b in reversed(extra_bits)] + ["y0", "c"]
    n = len(names)
    w_all = w_all.transpose(*[names.index(w) for w in wanted], n, n + 1)
    w_all = w_all.reshape(grp_size * seq_size, shard + small_rows, 3 * GROUP_WIDTH)
    small_all = w_all[:, shard:].reshape(grp_size * seq_size, -1)[:, : smalls.shape[0]]
    vectors = [small_all[:, i * shard : (i + 1) * shard].reshape(-1).astype(jnp.float32) for i in range(8)]
    q_bias, v_bias, o_bias, gain1, shift1, out_bias, gain2, shift2 = vectors
    in_bias = small_all[:, 8 * shard :].reshape(-1).astype(jnp.float32)
    w_all = w_all[:, :shard].reshape(width, 3 * GROUP_WIDTH)

    def own_columns(vector):
        return lax.dynamic_slice_in_dim(vector, head_group * GROUP_WIDTH, GROUP_WIDTH)

    qkv_bias = jnp.concatenate([own_columns(q_bias), jnp.zeros((GROUP_WIDTH,), jnp.float32), own_columns(v_bias)])
    qkv = dot(x_all, w_all) + qkv_bias
    queries = (qkv[:, :GROUP_WIDTH] * score_scale).astype(bf16)
    kv = qkv[:, GROUP_WIDTH:].astype(bf16)[None]
    for b in part_bits:
        bit = (me // b) % 2
        theirs = sflip(kv, b)
        kv = jnp.where(bit == 0, jnp.concatenate([kv, theirs]), jnp.concatenate([theirs, kv]))
    kv = kv.reshape(-1, 2 * GROUP_WIDTH)

    part = jnp.arange(n_parts, dtype=jnp.int32)
    part_device = part % 2 + 4 * (part // 2)
    member = jnp.arange(8, dtype=jnp.int32)
    member_device = (member // 4) * HI + ((member // 2) % 2) * ZO + (member % 2) * YO
    device = part_device[:, None] + member_device[None, :]
    position = (device[:, :, None] * rows + jnp.arange(rows, dtype=jnp.int32)).reshape(-1)
    bias = jnp.where(position < pick(valid_len, z1), 0.0, masked_score)[:, None]
    lane = jnp.arange(128, dtype=jnp.int32)[None, :]
    key_tail = jnp.where(lane == HEAD, bias, jnp.where((lane > HEAD) & (lane < HEAD + 4), 1.0, 0.0)).astype(bf16)

    context, context_full, stats = attend_forward(queries, kv, key_tail)

    teams = [
        [a * HI + b * ZO + c * YO + q for a in range(2) for b in range(2) for c in range(2)]
        for q in [i % 2 + 4 * (i // 2) for i in range(n_parts)]
    ]

    def exchange(blocks):
        return lax.all_to_all(blocks, "seq", 0, 0, axis_index_groups=teams, tiled=True)

    context = exchange(context.reshape(8, rows, GROUP_WIDTH))
    context = context.reshape(2, HEAD_GROUPS, rows, GROUP_WIDTH).transpose(0, 2, 1, 3).reshape(2 * rows, width)

    inner_lo = gathered_rows(0, 2 * shard).reshape(width, width)
    inner_hi = gathered_rows(2 * shard, 4 * shard).reshape(width, width)
    output_all = gathered_rows(4 * shard, first_end).reshape(width, width)
    outer_all = gathered_rows(first_end, first_end + outer_weight.shape[0])
    outer_all = outer_all.reshape(-1, 2, grp_size // 2, outer_weight.shape[0], width)
    outer_all = outer_all.transpose(0, 2, 1, 3, 4).reshape(half_feed, width)

    in_bias = pick(in_bias.reshape(chips, 2, piece).transpose(1, 0, 2).reshape(2, half_feed), core)

    home = tokens.reshape(2 * rows, width)
    cotangent = grad_out.reshape(2 * rows, width)
    hidden_one = home.astype(jnp.float32) + dot(context, output_all) + o_bias
    norm_one, norm_back_one = jax.vjp(layer_norm, hidden_one, gain1, shift1)
    first_out = norm_one.astype(bf16)
    n_own = 2 * rows
    both_first = jnp.concatenate([first_out, sflip(first_out, 1)], axis=0)

    def gelu_pair(pre):
        full, back = jax.vjp(partial(jax.nn.gelu, approximate=False), pre)
        return full.astype(bf16), back(jnp.ones_like(pre))[0]

    inner_all = jnp.concatenate([inner_lo, inner_hi], axis=1)
    active, slope = gelu_pair(dot(both_first, inner_all) + in_bias)
    outer_part = dot(active, outer_all)
    outer_sum = outer_part[:n_own] + sflip(outer_part[n_own:].astype(bf16), 1).astype(jnp.float32)
    hidden_two = first_out.astype(jnp.float32) + outer_sum + out_bias
    layer_out, norm_back_two = jax.vjp(layer_norm, hidden_two, gain2, shift2)
    dhidden_two, dsecond_gain, dsecond_shift = norm_back_two(cotangent.astype(jnp.float32))
    douter = dhidden_two.astype(bf16)
    both_douter = jnp.concatenate([douter, sflip(douter, 1)], axis=0)

    def over_chips(blocks):
        return lax.psum_scatter(blocks, "seq", scatter_dimension=0, tiled=False, axis_index_groups=chip_groups)

    def over_groups(blocks):
        for b in range(log2_of(grp_size)):
            blocks = (blocks.astype(jnp.float32) + flip(blocks, "grp", grp_size, 1 << b).astype(jnp.float32)).astype(bf16)
        return blocks

    dinner = (dot_t(both_douter, outer_all) * slope).astype(bf16)
    feed_blocks, dinner = lax.optimization_barrier(
        (feed_grads(both_first, dinner, active, both_douter, chips), dinner)
    )
    feed_sums = over_chips(feed_blocks)
    dfirst_part = dot_t(dinner, inner_all)
    dfirst = dhidden_two + dfirst_part[:n_own] + sflip(dfirst_part[n_own:].astype(bf16), 1).astype(jnp.float32)
    dhidden_one, dfirst_gain, dfirst_shift = norm_back_one(dfirst)
    dattend = dhidden_one.astype(bf16)
    dcontext = dot_t(dattend, output_all).astype(bf16)
    dcontext = dcontext.reshape(2, rows, HEAD_GROUPS, GROUP_WIDTH).transpose(0, 2, 1, 3)
    dcontext = exchange(dcontext.reshape(8, rows, GROUP_WIDTH)).reshape(8 * rows, GROUP_WIDTH)

    out_rows = width // seq_size
    ctx_split = context.reshape(n_own, chips, 2, out_rows)
    ctx_split = [ctx_split[:, :, i].reshape(n_own, width // 2) for i in range(2)]
    both_ctx = jnp.concatenate([pick(ctx_split, core), sflip(pick(ctx_split, 1 - core), 1)], axis=0)
    both_dattend = jnp.concatenate([dattend, sflip(dattend, 1)], axis=0)
    vectors = jnp.stack([dfirst_gain, dfirst_shift, dsecond_gain, dsecond_shift])
    other_blocks = other_grads(dinner, both_ctx, both_dattend, douter, vectors, chips)
    other_blocks, dcontext = lax.optimization_barrier((other_blocks, dcontext))

    last = part_bits[-1]
    dqueries, sent, kept = attend_backward(
        queries, kv, key_tail, context_full, stats, dcontext, ((me // last) % 2).astype(jnp.int32).reshape(1)
    )
    sent, feed_sums, other_blocks = lax.optimization_barrier((sent, feed_sums, other_blocks))
    other_sums = over_chips(other_blocks)
    dkv = (kept + sflip(sent, last).astype(jnp.float32)).reshape(n_parts // 2, 8 * rows, 2 * GROUP_WIDTH)
    for b in reversed(part_bits[:-1]):
        bit = (me // b) % 2
        n_now = dkv.shape[0] // 2
        low, high = dkv[:n_now], dkv[n_now:]
        sent = jnp.where(bit == 0, high, low).astype(bf16)
        dkv = jnp.where(bit == 0, low, high) + sflip(sent, b).astype(jnp.float32)
    dqkv = jnp.concatenate([dqueries, dkv[0].astype(bf16)], axis=1)

    dx = dot_t(dqkv, w_all).reshape(2, 2, 2, rows, width)
    da, db = dx[..., :half_width], dx[..., half_width:]

    def halve(low, high, bit, mask):
        sent = jnp.where(bit == 0, high, low).astype(bf16)
        return jnp.where(bit == 0, low, high) + sflip(sent, mask).astype(jnp.float32)

    da = halve(da[:, :, 0], da[:, :, 1], y0, YO)
    db = halve(db[:, 0], db[:, 1], z0, ZO)
    da = halve(da[:, 0], da[:, 1], z0, ZO)
    db = halve(db[:, 0], db[:, 1], y0, YO)
    dx = jnp.concatenate([da, db], axis=-1)
    dx, other_sums = lax.optimization_barrier((dx, other_sums))
    mine = pick(dx, z1)
    theirs = sflip(pick(dx, 1 - z1).astype(bf16), HI).astype(jnp.float32)
    dtokens = dhidden_one.reshape(2, rows, width) + in_order(mine, theirs, z1)

    feed_sums, other_sums = over_groups(feed_sums), over_groups(other_sums)
    r1 = 4 * out_rows
    inner_grad = feed_sums[:r1].reshape(2, 2, out_rows, width)
    inner_grad = [inner_grad[:, i] for i in range(2)]
    far = sflip(jnp.concatenate([pick(inner_grad, 1 - core).reshape(2 * out_rows, width), other_sums[out_rows:]], axis=0), 1)
    dinner_weight = in_order(pick(inner_grad, core), far[: 2 * out_rows].reshape(2, out_rows, width), core)
    dinner_weight = dinner_weight.transpose(2, 0, 1, 3).reshape(out_rows, 2, chips, piece).transpose(0, 2, 1, 3)
    dinner_weight = dinner_weight.reshape(out_rows, feed).astype(jnp.float32)
    douter_weight = feed_sums[r1:].astype(jnp.float32)
    doutput_weight = other_sums[:out_rows].astype(jnp.float32)
    small = other_sums[out_rows:].astype(jnp.float32)
    both = lax.dynamic_slice_in_dim(small + far[2 * out_rows :].astype(jnp.float32), me * out_rows, out_rows, axis=1)
    dfirst_gain, dfirst_shift, dsecond_gain, dsecond_shift, doutput_bias, douter_bias = (both[i] for i in range(6))
    dinner_bias = lax.dynamic_slice_in_dim(small[6:8].reshape(half_feed), (me // 2) * piece, piece)

    dw = t_dot(x_all, dqkv)
    dbias = column_sums(dqkv)
    dw = dw.reshape(seq_size, out_rows, 3 * GROUP_WIDTH)
    dw = jnp.concatenate([dw, jnp.broadcast_to(dbias, (seq_size, 8, 3 * GROUP_WIDTH))], axis=1)
    block = dw.shape[1]
    n_extra = 1 << len(extra_bits)
    dw = dw.reshape(2, 2, 2, n_extra, 2, 1, block, 3 * GROUP_WIDTH)[:, :, :, :, :, 0]
    dw = dw.reshape(2, 2, n_extra, 2, 2, block, 3 * GROUP_WIDTH)
    dw = halve(dw[:, :, :, :, 0], dw[:, :, :, :, 1], me % 2, 1)
    for b in reversed(extra_bits):
        m = dw.shape[2] // 2
        dw = halve(dw[:, :, :m], dw[:, :, m:], (me // b) % 2, b)
    dw = dw[:, :, 0]
    dw = halve(dw[0], dw[1], z1, HI)
    for b in range(log2_of(grp_size)):
        dw = dw + flip(dw.astype(bf16), "grp", grp_size, 1 << b).astype(jnp.float32)
    dw = dw.astype(bf16).reshape(HEAD_GROUPS, block, 3 * GROUP_WIDTH)

    def row_block(k):
        return lax.dynamic_index_in_dim(dw, head_group ^ k, 0, keepdims=False)

    w0 = row_block(0)
    w1 = sflip(row_block(1), YO)
    w2 = sflip(row_block(2), ZO)
    w3 = sflip(row_block(3), ZO | YO)
    dw = in_order(in_order(w0, w1, y0), in_order(w2, w3, y0), z0).reshape(HEAD_GROUPS, block, 3, GROUP_WIDTH)
    dw = dw.astype(jnp.float32).transpose(2, 1, 0, 3).reshape(3, block, width)
    dquery_weight, dkey_weight, dvalue_weight = dw[0, :out_rows], dw[1, :out_rows], dw[2, :out_rows]
    dquery_bias = lax.dynamic_slice_in_dim(dw[0, out_rows], me * out_rows, out_rows)
    dvalue_bias = lax.dynamic_slice_in_dim(dw[2, out_rows], me * out_rows, out_rows)

    return (
        layer_out.astype(bf16).reshape(2, rows, width),
        dtokens.astype(bf16),
        dquery_weight,
        dquery_bias,
        dkey_weight,
        dvalue_weight,
        dvalue_bias,
        doutput_weight,
        doutput_bias,
        dfirst_gain,
        dfirst_shift,
        dinner_weight,
        dinner_bias,
        douter_weight,
        douter_bias,
        dsecond_gain,
        dsecond_shift,
    )


def solution(mesh):
    in_specs = (
        P("grp", "seq", None),
        P("grp"),
        P(("grp", "seq"), None),
        P(("grp", "seq")),
        P(("grp", "seq"), None),
        P(("grp", "seq"), None),
        P(("grp", "seq")),
        P(("grp", "seq"), None),
        P(("grp", "seq")),
        P(("grp", "seq")),
        P(("grp", "seq")),
        P(("grp", "seq"), None),
        P(("grp", "seq")),
        P(("grp", "seq"), None),
        P(("grp", "seq")),
        P(("grp", "seq")),
        P(("grp", "seq")),
        P("grp", "seq", None),
    )
    out_specs = (
        P("grp", "seq", None),
        P("grp", "seq", None),
        P("seq", None),
        P("seq"),
        P("seq", None),
        P("seq", None),
        P("seq"),
        P("seq", None),
        P("seq"),
        P("seq"),
        P("seq"),
        P("seq", None),
        P("seq"),
        P("seq", None),
        P("seq"),
        P("seq"),
        P("seq"),
    )
    body = partial(per_device, mesh.shape["seq"], mesh.shape["grp"])
    return jax.shard_map(
        body, mesh=mesh, in_specs=in_specs, out_specs=out_specs, check_vma=False
    )
```

profile of v0, /device:TPU:0, one launch (start us, length us, event | category | flops | bytes accessed | tf_op | source)
XLA Modules:
  0.0 423.6 jit_solution(15904805760841730226)
XLA Ops:
  7.3 1.7 collective-permute-start.13
  10.8 3.5 collective-permute-start.12
  14.4 2.7 collective-permute-start
  22.1 8.5 %collective-permute-done = bf16[192,768]{1,0:T(8,128)(2,1)S(1)} collective-permute-done((bf16[192,768]{1,0:T(8,128)(2,1)S(1)}, bf16[192,768]{1,0:T(8,128)(2,1)S(1)}, u32[]{:S(2)}, u32[]{:S(2)}) %collective-permute-start) | collective-permute-done | bytes 294944 | tf_op jit(solution)/shard_map/ppermute | solution.py:28
  31.2 1.6 collective-permute-start.6
  34.5 2.1 collective-permute-start.3
  37.9 2.4 collective-permute-done.6
  40.3 1.6 collective-permute-start.8
  42.1 10.6 %collective-permute-done.8 = bf16[2,2,32,576]{3,2,1,0:T(8,128)(2,1)S(1)} collective-permute-done((bf16[2,2,32,576]{3,2,1,0:T(8,128)(2,1)S(1)}, bf16[2,2,32,576]{3,2,1,0:T(8,128)(2,1)S(1)}, u32[]{:S(2)}, u32[]{:S(2)}) %collective-permute-start.8) | collective-permute-done | bytes 147488 | tf_op jit(solution)/shard_map/ppermute | solution.py:28
  52.8 1.7 collective-permute-start.9
  54.8 4.4 %collective-permute-start.2 = (bf16[2,2,192,384]{3,2,1,0:T(8,128)(2,1)S(1)}, bf16[2,2,192,384]{3,2,1,0:T(8,128)(2,1)S(1)}, u32[]{:S(2)}, u32[]{:S(2)}) collective-permute-start(bf16[2,2,192,384]{3,2,1,0:T(8,128)(2,1)S(1)} %maximum_select_fusion.12), channel_id=1, source_target_pairs={{0,4},{1,5},{2,6},{3,7},{4,0},{5,1},{6,2},{7,3},{8,12},{9,13},{10,... | collective-permute-start | bytes 1769480 | tf_op jit(solution)/shard_map/ppermute | solution.py:28
  62.3 24.4 %collective-permute-done.2 = bf16[2,2,192,384]{3,2,1,0:T(8,128)(2,1)S(1)} collective-permute-done((bf16[2,2,192,384]{3,2,1,0:T(8,128)(2,1)S(1)}, bf16[2,2,192,384]{3,2,1,0:T(8,128)(2,1)S(1)}, u32[]{:S(2)}, u32[]{:S(2)}) %collective-permute-start.2) | collective-permute-done | bytes 589856 | tf_op jit(solution)/shard_map/ppermute | solution.py:28
  92.3 3.2 convolution_add_fusion
  98.9 1.8 maximum_select_fusion
  101.2 28.3 %attend_forward.1 = (bf16[1536,192]{1,0:T(8,128)(2,1)}, f32[1536,192]{1,0:T(8,128)}, f32[1536,128]{1,0:T(8,128)}) custom-call(bf16[1536,192]{1,0:T(8,128)(2,1)} %fusion.8.q_ref, bf16[3072,384]{1,0:T(8,128)(2,1)} %bitcast.310, bf16[3072,128]{1,0:T(8,128)(2,1)} %select_convert_fusion.kb_ref), custom_call_target="tpu_custom_call" | custom-call | flops 14495514624 | bytes 18874368 | tf_op jit(solution)/shard_map/attend_forward/pallas_call | solution.py:103
  129.5 3.5 all-to-all-start
  134.3 19.1 %all-to-all-done = bf16[8,192,192]{2,1,0:T(8,128)(2,1)S(1)} async-done(((bf16[8,192,192]{2,1,0:T(8,128)(2,1)}), bf16[8,192,192]{2,1,0:T(8,128)(2,1)S(1)}, u32[]{:S(2)}, u32[]{:S(2)}) %all-to-all-start) | async-done | bytes 589856 | tf_op jit(solution)/shard_map/all_to_all | solution.py:410
  154.7 1.5 slice_bitcast_fusion.7
  157.6 9.3 %collective-permute-done.14 = bf16[8,240,768]{2,1,0:T(8,128)(2,1)} collective-permute-done((bf16[8,240,768]{2,1,0:T(8,128)(2,1)}, bf16[8,240,768]{2,1,0:T(8,128)(2,1)}, u32[]{:S(2)}, u32[]{:S(2)}) %collective-permute-start.14) | collective-permute-done | bytes 2949152 | tf_op jit(solution)/shard_map/ppermute | solution.py:28
  172.6 14.6 %multiply_convert_fusion.1 = (bf16[768,1536]{1,0:T(8,128)(2,1)S(1)}, f32[768,1536]{1,0:T(8,128)}, f32[768,1536]{1,0:T(8,128)}) fusion(f32[1536]{0:T(1024)S(1)} %select_n.792, bf16[768,768]{1,0:T(8,128)(2,1)S(1)} %bitcast.337, bf16[768,768]{1,0:T(8,128)(2,1)S(1)} %bitcast.335, bf16[384,768]{1,0:T(8,128)(2,1)S(1)} %collective-permute-done.15, ...), kind=kOutput, calls=%fused_computation.3 | convolution fusion | flops 1896873984 | bytes 15341568 | tf_op jit(solution)/shard_map/dot_general | solution.py:46
  187.3 2.0 fusion.74
  192.9 1.9 fusion.64
  202.5 4.7 %multiply_convert_fusion.dz_ref = bf16[768,1536]{1,0:T(8,128)(2,1)} fusion(f32[768,1536]{1,0:T(8,128)S(1)} %copy-done.41, f32[768,1536]{1,0:T(8,128)S(1)} %copy-done.42, bf16[1536,768]{1,0:T(8,128)(2,1)S(1)} %bitcast.327, f32[1536]{0:T(1024)S(1)} %select_n.792, bf16[384,768]{1,0:T(8,128)(2,1)S(1)} %collective-permute-done.17, ...), kind=kOutput, calls=%fused_computation.2 | convolution fusion | flops 1829634048 | bytes 15341568 | tf_op jit(solution)/shard_map/dot_general | solution.py:50
  207.3 9.0 %feed_grads.1 = bf16[8,384,768]{2,1,0:T(8,128)(2,1)} custom-call(bf16[768,768]{1,0:T(8,128)(2,1)} %pad_maximum_fusion.6.y_ref, bf16[768,1536]{1,0:T(8,128)(2,1)} %multiply_convert_fusion.dz_ref, bf16[768,1536]{1,0:T(8,128)(2,1)} %copy-done.40, bf16[768,768]{1,0:T(8,128)(2,1)} %pad_maximum_fusion.7.do_ref), custom_call_target="tpu_custom_call" | custom-call | flops 3623878656 | bytes 11796480 | tf_op jit(solution)/shard_map/feed_grads/pallas_call | solution.py:206
  216.3 4.4 %fusion.9 = f32[768,768]{1,0:T(8,128)S(1)} fusion(bf16[768,1536]{1,0:T(8,128)(2,1)} %multiply_convert_fusion.dz_ref, bf16[768,768]{1,0:T(8,128)(2,1)} %bitcast.338, bf16[768,768]{1,0:T(8,128)(2,1)} %bitcast.336), kind=kOutput, calls=%fused_computation.34 | convolution fusion | flops 1816657920 | bytes 7077888 | tf_op jit(solution)/shard_map/dot_general | solution.py:50
  221.2 1.6 collective-permute-done.18
  228.1 3.5 all-to-all-start.1
  236.9 2.1 pad_maximum_fusion.8.da_ref
  239.1 4.4 %other_grads.1 = bf16[8,56,768]{2,1,0:T(8,128)(2,1)} custom-call(bf16[768,1536]{1,0:T(8,128)(2,1)} %multiply_convert_fusion.dz_ref, bf16[768,384]{1,0:T(8,128)(2,1)} %pad_maximum_fusion.10.ctx_ref, bf16[768,768]{1,0:T(8,128)(2,1)} %pad_maximum_fusion.8.da_ref, bf16[384,768]{1,0:T(8,128)(2,1)} %copy-done.2, f32[4,768]{1,0:T(4,128)} %pad_maximum_fusion.15.vec_ref), custom_call_target="tpu_custom_call" | custom-call | flops 452984832 | bytes 5898240 | tf_op jit(solution)/shard_map/other_grads/pallas_call | solution.py:232
  243.4 28.9 %all-to-all-done.1 = bf16[8,192,192]{2,1,0:T(8,128)(2,1)S(1)} async-done(((bf16[8,192,192]{2,1,0:T(8,128)(2,1)}), bf16[8,192,192]{2,1,0:T(8,128)(2,1)S(1)}, u32[]{:S(2)}, u32[]{:S(2)}) %all-to-all-start.1) | async-done | bytes 589856 | tf_op jit(solution)/shard_map/all_to_all | solution.py:410
  273.3 43.9 %attend_backward.1 = (bf16[1536,192]{1,0:T(8,128)(2,1)}, bf16[1536,384]{1,0:T(8,128)(2,1)}, f32[1536,384]{1,0:T(8,128)}) custom-call(s32[1]{0:T(128)} %bitcast.73.bit_ref, bf16[1536,192]{1,0:T(8,128)(2,1)} %fusion.8.q_ref, bf16[3072,384]{1,0:T(8,128)(2,1)} %bitcast.311, bf16[3072,128]{1,0:T(8,128)(2,1)} %select_convert_fusion.kb_ref, ...), custom_call_target="tpu_custom_call" | custom-call | tf_op jit(solution)/shard_map/attend_backward/pallas_call | solution.py:176
  317.2 9.1 %reduce-scatter.3.cloned.1.call-done = bf16[1,384,768]{2,1,0:T(8,128)(2,1)} async-done(((bf16[8,384,768]{2,1,0:T(8,128)(2,1)}), bf16[1,384,768]{2,1,0:T(8,128)(2,1)}) %reduce-scatter.3.cloned.1.call-update) | async-done | bytes 589840 | tf_op jit(solution)/shard_map/reduce_scatter | solution.py:447
  327.8 2.7 copy.138
  330.6 10.9 %collective-permute-done.34 = bf16[384,768]{1,0:T(8,128)(2,1)} collective-permute-done((bf16[384,768]{1,0:T(8,128)(2,1)}, bf16[384,768]{1,0:T(8,128)(2,1)}, u32[]{:S(2)}, u32[]{:S(2)}) %collective-permute-start.34) | collective-permute-done | bytes 589856 | tf_op jit(solution)/shard_map/ppermute | solution.py:28
  349.2 2.1 fusion.6
  352.7 2.0 fusion.75
  354.9 1.6 collective-permute-start.24
  358.4 1.7 collective-permute-start.28
  360.1 16.1 %collective-permute-done.24 = bf16[2,2,192,384]{3,2,1,0:T(8,128)(2,1)S(1)} collective-permute-done((bf16[2,2,192,384]{3,2,1,0:T(8,128)(2,1)S(1)}, bf16[2,2,192,384]{3,2,1,0:T(8,128)(2,1)S(1)}, u32[]{:S(2)}, u32[]{:S(2)}) %collective-permute-start.24) | collective-permute-done | bytes 589856 | tf_op jit(solution)/shard_map/ppermute | solution.py:28
  376.6 1.5 collective-permute-start.25
  380.7 4.7 %collective-permute-done.25 = bf16[2,192,384]{2,1,0:T(8,128)(2,1)S(1)} collective-permute-done((bf16[2,192,384]{2,1,0:T(8,128)(2,1)S(1)}, bf16[2,192,384]{2,1,0:T(8,128)(2,1)S(1)}, u32[]{:S(2)}, u32[]{:S(2)}) %collective-permute-start.25) | collective-permute-done | bytes 294944 | tf_op jit(solution)/shard_map/ppermute | solution.py:28
  385.5 2.4 collective-permute-done.23
  388.1 3.5 reduce-scatter.5.cloned.1.call-done
  391.6 1.6 collective-permute-start.33
  394.7 1.6 collective-permute-done.33
  398.2 2.1 collective-permute-start.32
  403.5 4.9 %collective-permute-done.31 = bf16[56,576]{1,0:T(8,128)(2,1)S(1)} collective-permute-done((bf16[56,576]{1,0:T(8,128)(2,1)S(1)}, bf16[56,576]{1,0:T(8,128)(2,1)S(1)}, u32[]{:S(2)}, u32[]{:S(2)}) %collective-permute-start.31) | collective-permute-done | bytes 64544 | tf_op jit(solution)/shard_map/ppermute | solution.py:28
  413.4 1.6 reshape.1385
  (324 shorter events, 83.4 us)
Async XLA Ops:
  7.2 93.5 %all-gather.3.cloned.1.call-start = ((), (), s32[]{:S(2)}) async-start(), calls=%async_computation.6 | async-start | bytes 3317760 | tf_op jit(solution)/shard_map/all_gather | solution.py:321
  7.3 14.0 %collective-permute-start.13 = (bf16[96,768]{1,0:T(8,128)(2,1)}, bf16[96,768]{1,0:T(8,128)(2,1)S(1)}, u32[]{:S(2)}, u32[]{:S(2)}) collective-permute-start(bf16[96,768]{1,0:T(8,128)(2,1)} %param.33), channel_id=1, source_target_pairs={{0,0},{1,2},{2,1},{3,3},{4,4},{5,6},{6,5},{7,7},{8,8},{9,10},{10,9... | collective-permute-start | bytes 442376 | tf_op jit(solution)/shard_map/ppermute | solution.py:306
  10.5 9.2 %copy-start.28 = (bf16[24,768]{1,0:T(8,128)(2,1)S(1)}, bf16[24,768]{1,0:T(8,128)(2,1)}, u32[]{:S(2)}) copy-start(bf16[24,768]{1,0:T(8,128)(2,1)} %param.24) | copy-start | bytes 110596
  10.6 9.3 %copy-start.29 = (bf16[24,768]{1,0:T(8,128)(2,1)S(1)}, bf16[24,768]{1,0:T(8,128)(2,1)}, u32[]{:S(2)}) copy-start(bf16[24,768]{1,0:T(8,128)(2,1)} %param.25) | copy-start | bytes 110596
  10.8 10.1 %collective-permute-start.12 = (bf16[72,768]{1,0:T(8,128)(2,1)S(1)}, bf16[72,768]{1,0:T(8,128)(2,1)S(1)}, u32[]{:S(2)}, u32[]{:S(2)}) collective-permute-start(bf16[72,768]{1,0:T(8,128)(2,1)S(1)} %pad_maximum_fusion.14), channel_id=1, source_target_pairs={{0,1},{1,0},{2,3},{3,2},{4,5},{5,4},{6,7},{7,6},{8,9},{9,8},{10,11... | collective-permute-start | bytes 331784 | tf_op jit(solution)/shard_map/ppermute | solution.py:28
  14.4 16.2 %collective-permute-start = (bf16[192,768]{1,0:T(8,128)(2,1)S(1)}, bf16[192,768]{1,0:T(8,128)(2,1)S(1)}, u32[]{:S(2)}, u32[]{:S(2)}) collective-permute-start(bf16[192,768]{1,0:T(8,128)(2,1)S(1)} %get-tuple-element.97), channel_id=1, source_target_pairs={{0,8},{1,9},{2,10},{3,11},{4,12},{5,13},{6,14},{7,15},{8,0},{9,1},... | collective-permute-start | bytes 884744 | tf_op jit(solution)/shard_map/ppermute | solution.py:28
  30.6 7.3 %collective-permute-start.7 = (bf16[32,576]{1,0:T(8,128)(2,1)S(1)}, bf16[32,576]{1,0:T(8,128)(2,1)S(1)}, u32[]{:S(2)}, u32[]{:S(2)}) collective-permute-start(bf16[32,576]{1,0:T(8,128)(2,1)S(1)} %get-tuple-element.124), channel_id=1, source_target_pairs={{0,6},{1,7},{2,4},{3,5},{4,2},{5,3},{6,0},{7,1},{8,14},{9,15},{10,... | collective-permute-start | bytes 110600 | tf_op jit(solution)/shard_map/ppermute | solution.py:28
  31.2 9.1 %collective-permute-start.6 = (bf16[32,576]{1,0:T(8,128)(2,1)S(1)}, bf16[32,576]{1,0:T(8,128)(2,1)S(1)}, u32[]{:S(2)}, u32[]{:S(2)}) collective-permute-start(bf16[32,576]{1,0:T(8,128)(2,1)S(1)} %get-tuple-element.125), channel_id=1, source_target_pairs={{0,4},{1,5},{2,6},{3,7},{4,0},{5,1},{6,2},{7,3},{8,12},{9,13},{10,... | collective-permute-start | bytes 110600 | tf_op jit(solution)/shard_map/ppermute | solution.py:28
  32.8 4.2 collective-permute-start.5
  34.5 24.7 %collective-permute-start.3 = (bf16[2,192,384]{2,1,0:T(8,128)(2,1)S(1)}, bf16[2,192,384]{2,1,0:T(8,128)(2,1)S(1)}, u32[]{:S(2)}, u32[]{:S(2)}) collective-permute-start(bf16[2,192,384]{2,1,0:T(8,128)(2,1)S(1)} %get-tuple-element.94), channel_id=1, source_target_pairs={{0,4},{1,5},{2,6},{3,7},{4,0},{5,1},{6,2},{7,3},{8,12},{9,13},{10,... | collective-permute-start | bytes 884744 | tf_op jit(solution)/shard_map/ppermute | solution.py:28
  36.6 18.1 %collective-permute-start.1 = (bf16[2,192,384]{2,1,0:T(8,128)(2,1)S(1)}, bf16[2,192,384]{2,1,0:T(8,128)(2,1)S(1)}, u32[]{:S(2)}, u32[]{:S(2)}) collective-permute-start(bf16[2,192,384]{2,1,0:T(8,128)(2,1)S(1)} %get-tuple-element.95), channel_id=1, source_target_pairs={{0,2},{1,3},{2,0},{3,1},{4,6},{5,7},{6,4},{7,5},{8,10},{9,11},{10,... | collective-permute-start | bytes 884744 | tf_op jit(solution)/shard_map/ppermute | solution.py:28
  40.3 12.3 %collective-permute-start.8 = (bf16[2,2,32,576]{3,2,1,0:T(8,128)(2,1)S(1)}, bf16[2,2,32,576]{3,2,1,0:T(8,128)(2,1)S(1)}, u32[]{:S(2)}, u32[]{:S(2)}) collective-permute-start(bf16[2,2,32,576]{3,2,1,0:T(8,128)(2,1)S(1)} %maximum_select_fusion.19), channel_id=1, source_target_pairs={{0,8},{1,9},{2,10},{3,11},{4,12},{5,13},{6,14},{7,15},{8,0},{9,1},... | collective-permute-start | bytes 442376 | tf_op jit(solution)/shard_map/ppermute | solution.py:28
  52.8 9.0 %collective-permute-start.9 = (bf16[2,2,2,32,576]{4,3,2,1,0:T(8,128)(2,1)S(1)}, bf16[2,2,2,32,576]{4,3,2,1,0:T(8,128)(2,1)S(1)}, u32[]{:S(2)}, u32[]{:S(2)}) collective-permute-start(bf16[2,2,2,32,576]{4,3,2,1,0:T(8,128)(2,1)S(1)} %maximum_select_fusion.16), channel_id=1, source_target_pairs={{0,16},{16,0},{1,17},{17,1},{2,18},{18,2},{3,19},{19,3},{4,20},{20... | collective-permute-start | bytes 884744 | tf_op jit(solution)/shard_map/ppermute | solution.py:28
  54.8 31.9 %collective-permute-start.2 = (bf16[2,2,192,384]{3,2,1,0:T(8,128)(2,1)S(1)}, bf16[2,2,192,384]{3,2,1,0:T(8,128)(2,1)S(1)}, u32[]{:S(2)}, u32[]{:S(2)}) collective-permute-start(bf16[2,2,192,384]{3,2,1,0:T(8,128)(2,1)S(1)} %maximum_select_fusion.12), channel_id=1, source_target_pairs={{0,4},{1,5},{2,6},{3,7},{4,0},{5,1},{6,2},{7,3},{8,12},{9,13},{10,... | collective-permute-start | bytes 1769480 | tf_op jit(solution)/shard_map/ppermute | solution.py:28
  59.3 28.3 %collective-permute-start.4 = (bf16[2,2,192,384]{3,2,1,0:T(8,128)(2,1)S(1)}, bf16[2,2,192,384]{3,2,1,0:T(8,128)(2,1)S(1)}, u32[]{:S(2)}, u32[]{:S(2)}) collective-permute-start(bf16[2,2,192,384]{3,2,1,0:T(8,128)(2,1)S(1)} %maximum_select_fusion.14), channel_id=1, source_target_pairs={{0,2},{1,3},{2,0},{3,1},{4,6},{5,7},{6,4},{7,5},{8,10},{9,11},{10,... | collective-permute-start | bytes 1769480 | tf_op jit(solution)/shard_map/ppermute | solution.py:28
  61.9 26.2 %collective-permute-start.10 = (bf16[2,2,2,2,32,576]{5,4,3,2,1,0:T(8,128)(2,1)S(1)}, bf16[2,2,2,2,32,576]{5,4,3,2,1,0:T(8,128)(2,1)S(1)}, u32[]{:S(2)}, u32[]{:S(2)}) collective-permute-start(bf16[2,2,2,2,32,576]{5,4,3,2,1,0:T(8,128)(2,1)S(1)} %maximum_select_fusion.10), channel_id=1, source_target_pairs={{0,1},{1,0},{2,3},{3,2},{4,5},{5,4},{6,7},{7,6},{8,9},{9,8},{10,11... | collective-permute-start | bytes 1769480 | tf_op jit(solution)/shard_map/ppermute | solution.py:28
  95.9 2.9 collective-permute-start.11
  100.7 66.2 %collective-permute-start.14 = (bf16[8,240,768]{2,1,0:T(8,128)(2,1)}, bf16[8,240,768]{2,1,0:T(8,128)(2,1)}, u32[]{:S(2)}, u32[]{:S(2)}) collective-permute-start(bf16[8,240,768]{2,1,0:T(8,128)(2,1)} %bitcast.323), channel_id=1, source_target_pairs={{0,16},{16,0},{1,17},{17,1},{2,18},{18,2},{3,19},{19,3},{4,20},{20... | collective-permute-start | bytes 8847368 | tf_op jit(solution)/shard_map/ppermute | solution.py:28
  129.5 23.9 %all-to-all-start = ((bf16[8,192,192]{2,1,0:T(8,128)(2,1)}), bf16[8,192,192]{2,1,0:T(8,128)(2,1)S(1)}, u32[]{:S(2)}, u32[]{:S(2)}) async-start(bf16[8,192,192]{2,1,0:T(8,128)(2,1)} %bitcast.351), calls=%async_computation | async-start | bytes 1572864 | tf_op jit(solution)/shard_map/all_to_all | solution.py:410
  133.0 193.3 %reduce-scatter.3.cloned.1.call-start = ((), (), s32[]{:S(2)}) async-start(), calls=%async_computation.4 | async-start | bytes 5308416 | tf_op jit(solution)/shard_map/reduce_scatter | solution.py:447
  170.2 2.4 collective-permute-start.15
  172.2 15.1 %copy-start.8 = (bf16[2,8,96,768]{3,2,1,0:T(8,128)(2,1)}, bf16[2,8,96,768]{3,2,1,0:T(8,128)(2,1)S(1)}, u32[]{:S(2)}) copy-start(bf16[2,8,96,768]{3,2,1,0:T(8,128)(2,1)S(1)} %maximum_select_fusion.1) | copy-start | bytes 7077892
  172.6 14.7 %copy-start.15 = (bf16[2,8,48,768]{3,2,1,0:T(8,128)(2,1)}, bf16[2,8,48,768]{3,2,1,0:T(8,128)(2,1)S(1)}, u32[]{:S(2)}) copy-start(bf16[2,8,48,768]{3,2,1,0:T(8,128)(2,1)S(1)} %get-tuple-element.140) | copy-start | bytes 3538948
  172.6 14.7 %copy-start.16 = (bf16[2,8,48,768]{3,2,1,0:T(8,128)(2,1)}, bf16[2,8,48,768]{3,2,1,0:T(8,128)(2,1)S(1)}, u32[]{:S(2)}) copy-start(bf16[2,8,48,768]{3,2,1,0:T(8,128)(2,1)S(1)} %get-tuple-element.141) | copy-start | bytes 3538948
  172.6 14.7 %copy-start.22 = (bf16[384,768]{1,0:T(8,128)(2,1)}, bf16[384,768]{1,0:T(8,128)(2,1)S(1)}, u32[]{:S(2)}) copy-start(bf16[384,768]{1,0:T(8,128)(2,1)S(1)} %collective-permute-done.15) | copy-start | bytes 1769476
  190.8 2.1 collective-permute-start.16
  198.0 2.4 collective-permute-start.17
  220.8 2.1 collective-permute-start.18
  228.1 44.2 %all-to-all-start.1 = ((bf16[8,192,192]{2,1,0:T(8,128)(2,1)}), bf16[8,192,192]{2,1,0:T(8,128)(2,1)S(1)}, u32[]{:S(2)}, u32[]{:S(2)}) async-start(bf16[8,192,192]{2,1,0:T(8,128)(2,1)} %bitcast.78), calls=%async_computation.1 | async-start | bytes 1572864 | tf_op jit(solution)/shard_map/all_to_all | solution.py:410
  231.6 160.0 %reduce-scatter.5.cloned.1.call-start = ((), (), s32[]{:S(2)}) async-start(), calls=%async_computation.5 | async-start | bytes 774144 | tf_op jit(solution)/shard_map/reduce_scatter | solution.py:447
  232.9 4.0 collective-permute-start.20
  233.6 1.8 collective-permute-start.19
  273.3 54.5 %copy-start.1 = (bf16[2,2,2,192,768]{4,3,2,1,0:T(8,128)(2,1)S(1)}, bf16[2,2,2,192,768]{4,3,2,1,0:T(8,128)(2,1)}, u32[]{:S(2)}) copy-start(bf16[2,2,2,192,768]{4,3,2,1,0:T(8,128)(2,1)} %copy-done) | copy-start | bytes 7077892
  326.3 15.1 %collective-permute-start.34 = (bf16[384,768]{1,0:T(8,128)(2,1)}, bf16[384,768]{1,0:T(8,128)(2,1)}, u32[]{:S(2)}, u32[]{:S(2)}) collective-permute-start(bf16[384,768]{1,0:T(8,128)(2,1)} %bitcast.354), channel_id=1, source_target_pairs={{0,16},{16,0},{1,17},{17,1},{2,18},{18,2},{3,19},{19,3},{4,20},{20... | collective-permute-start | bytes 1769480 | tf_op jit(solution)/shard_map/ppermute | solution.py:28
  327.8 17.6 %collective-permute-start.21 = (bf16[1536,384]{1,0:T(8,128)(2,1)}, bf16[1536,384]{1,0:T(8,128)(2,1)S(1)}, u32[]{:S(2)}, u32[]{:S(2)}) collective-permute-start(bf16[1536,384]{1,0:T(8,128)(2,1)} %get-tuple-element.56), channel_id=1, source_target_pairs={{0,1},{1,0},{2,3},{3,2},{4,5},{5,4},{6,7},{7,6},{8,9},{9,8},{10,11... | collective-permute-start | bytes 3538952 | tf_op jit(solution)/shard_map/ppermute | solution.py:28
  351.6 6.6 %collective-permute-start.27 = (bf16[2,2,1,2,56,576]{5,4,3,1,0,2:T(8,128)(2,1)S(1)}, bf16[2,2,1,2,56,576]{5,4,3,1,0,2:T(8,128)(2,1)S(1)}, u32[]{:S(2)}, u32[]{:S(2)}) collective-permute-start(bf16[2,2,1,2,56,576]{5,4,3,1,0,2:T(8,128)(2,1)S(1)} %fusion.34), channel_id=1, source_target_pairs={{0,1},{1,0},{2,3},{3,2},{4,5},{5,4},{6,7},{7,6},{8,9},{9,8},{10,11... | collective-permute-start | bytes 1548296 | tf_op jit(solution)/shard_map/ppermute | solution.py:28
  354.9 21.4 %collective-permute-start.24 = (bf16[2,2,192,384]{3,2,1,0:T(8,128)(2,1)S(1)}, bf16[2,2,192,384]{3,2,1,0:T(8,128)(2,1)S(1)}, u32[]{:S(2)}, u32[]{:S(2)}) collective-permute-start(bf16[2,2,192,384]{3,2,1,0:T(8,128)(2,1)S(1)} %fusion.30), channel_id=1, source_target_pairs={{0,4},{1,5},{2,6},{3,7},{4,0},{5,1},{6,2},{7,3},{8,12},{9,13},{10,... | collective-permute-start | bytes 1769480 | tf_op jit(solution)/shard_map/ppermute | solution.py:28
  356.7 21.4 %collective-permute-start.22 = (bf16[2,2,192,384]{3,2,0,1:T(8,128)(2,1)S(1)}, bf16[2,2,192,384]{3,2,0,1:T(8,128)(2,1)S(1)}, u32[]{:S(2)}, u32[]{:S(2)}) collective-permute-start(bf16[2,2,192,384]{3,2,0,1:T(8,128)(2,1)S(1)} %fusion.29), channel_id=1, source_target_pairs={{0,2},{1,3},{2,0},{3,1},{4,6},{5,7},{6,4},{7,5},{8,10},{9,11},{10,... | collective-permute-start | bytes 1769480 | tf_op jit(solution)/shard_map/ppermute | solution.py:28
  358.4 20.0 %collective-permute-start.28 = (bf16[2,2,56,576]{3,2,1,0:T(8,128)(2,1)S(1)}, bf16[2,2,56,576]{3,2,1,0:T(8,128)(2,1)S(1)}, u32[]{:S(2)}, u32[]{:S(2)}) collective-permute-start(bf16[2,2,56,576]{3,2,1,0:T(8,128)(2,1)S(1)} %fusion.39), channel_id=1, source_target_pairs={{0,8},{1,9},{2,10},{3,11},{4,12},{5,13},{6,14},{7,15},{8,0},{9,1},... | collective-permute-start | bytes 774152 | tf_op jit(solution)/shard_map/ppermute | solution.py:28
  376.6 8.9 %collective-permute-start.25 = (bf16[2,192,384]{2,1,0:T(8,128)(2,1)S(1)}, bf16[2,192,384]{2,1,0:T(8,128)(2,1)S(1)}, u32[]{:S(2)}, u32[]{:S(2)}) collective-permute-start(bf16[2,192,384]{2,1,0:T(8,128)(2,1)S(1)} %fusion.37), channel_id=1, source_target_pairs={{0,2},{1,3},{2,0},{3,1},{4,6},{5,7},{6,4},{7,5},{8,10},{9,11},{10,... | collective-permute-start | bytes 884744 | tf_op jit(solution)/shard_map/ppermute | solution.py:28
  378.4 9.6 %collective-permute-start.23 = (bf16[2,192,384]{2,1,0:T(8,128)(2,1)S(1)}, bf16[2,192,384]{2,1,0:T(8,128)(2,1)S(1)}, u32[]{:S(2)}, u32[]{:S(2)}) collective-permute-start(bf16[2,192,384]{2,1,0:T(8,128)(2,1)S(1)} %fusion.36), channel_id=1, source_target_pairs={{0,4},{1,5},{2,6},{3,7},{4,0},{5,1},{6,2},{7,3},{8,12},{9,13},{10,... | collective-permute-start | bytes 884744 | tf_op jit(solution)/shard_map/ppermute | solution.py:28
  379.2 17.8 %collective-permute-start.29 = (bf16[2,2,56,576]{3,2,1,0:T(8,128)(2,1)}, bf16[2,2,56,576]{3,2,1,0:T(8,128)(2,1)}, u32[]{:S(2)}, u32[]{:S(2)}) collective-permute-start(bf16[2,2,56,576]{3,2,1,0:T(8,128)(2,1)} %fusion.45), channel_id=1, source_target_pairs={{0,16},{16,0},{1,17},{17,1},{2,18},{18,2},{3,19},{19,3},{4,20},{20... | collective-permute-start | bytes 774152 | tf_op jit(solution)/shard_map/ppermute | solution.py:28
  391.6 4.7 %collective-permute-start.33 = (bf16[56,768]{1,0:T(8,128)(2,1)}, bf16[56,768]{1,0:T(8,128)(2,1)S(1)}, u32[]{:S(2)}, u32[]{:S(2)}) collective-permute-start(bf16[56,768]{1,0:T(8,128)(2,1)} %bitcast.375), channel_id=1, source_target_pairs={{0,16},{16,0},{1,17},{17,1},{2,18},{18,2},{3,19},{19,3},{4,20},{20... | collective-permute-start | bytes 258056 | tf_op jit(solution)/shard_map/ppermute | solution.py:28
  393.4 22.2 %collective-permute-start.26 = (bf16[192,768]{1,0:T(8,128)(2,1)S(1)}, bf16[192,768]{1,0:T(8,128)(2,1)S(1)}, u32[]{:S(2)}, u32[]{:S(2)}) collective-permute-start(bf16[192,768]{1,0:T(8,128)(2,1)S(1)} %fusion.38), channel_id=1, source_target_pairs={{0,8},{1,9},{2,10},{3,11},{4,12},{5,13},{6,14},{7,15},{8,0},{9,1},... | collective-permute-start | bytes 884744 | tf_op jit(solution)/shard_map/ppermute | solution.py:28
  398.2 5.3 %collective-permute-start.32 = (bf16[56,576]{1,0:T(8,128)(2,1)S(1)}, bf16[56,576]{1,0:T(8,128)(2,1)S(1)}, u32[]{:S(2)}, u32[]{:S(2)}) collective-permute-start(bf16[56,576]{1,0:T(8,128)(2,1)S(1)} %get-tuple-element.118), channel_id=1, source_target_pairs={{0,6},{1,7},{2,4},{3,5},{4,2},{5,3},{6,0},{7,1},{8,14},{9,15},{10,... | collective-permute-start | bytes 193544 | tf_op jit(solution)/shard_map/ppermute | solution.py:28
  400.3 8.1 %collective-permute-start.31 = (bf16[56,576]{1,0:T(8,128)(2,1)S(1)}, bf16[56,576]{1,0:T(8,128)(2,1)S(1)}, u32[]{:S(2)}, u32[]{:S(2)}) collective-permute-start(bf16[56,576]{1,0:T(8,128)(2,1)S(1)} %get-tuple-element.119), channel_id=1, source_target_pairs={{0,4},{1,5},{2,6},{3,7},{4,0},{5,1},{6,2},{7,3},{8,12},{9,13},{10,... | collective-permute-start | bytes 193544 | tf_op jit(solution)/shard_map/ppermute | solution.py:28
  400.7 11.2 %collective-permute-start.35 = (bf16[104,768]{1,0:T(8,128)(2,1)S(1)}, bf16[104,768]{1,0:T(8,128)(2,1)S(1)}, u32[]{:S(2)}, u32[]{:S(2)}) collective-permute-start(bf16[104,768]{1,0:T(8,128)(2,1)S(1)} %pad_maximum_fusion.13), channel_id=1, source_target_pairs={{0,1},{1,0},{2,3},{3,2},{4,5},{5,4},{6,7},{7,6},{8,9},{9,8},{10,11... | collective-permute-start | bytes 479240 | tf_op jit(solution)/shard_map/ppermute | solution.py:28
  401.4 7.1 %collective-permute-start.30 = (bf16[56,576]{1,0:T(8,128)(2,1)S(1)}, bf16[56,576]{1,0:T(8,128)(2,1)S(1)}, u32[]{:S(2)}, u32[]{:S(2)}) collective-permute-start(bf16[56,576]{1,0:T(8,128)(2,1)S(1)} %get-tuple-element.120), channel_id=1, source_target_pairs={{0,2},{1,3},{2,0},{3,1},{4,6},{5,7},{6,4},{7,5},{8,10},{9,11},{10,... | collective-permute-start | bytes 193544 | tf_op jit(solution)/shard_map/ppermute | solution.py:28
  (36 other events, 163.7 us)
Sparse Core Ops, SparseCore 0:
  22.2 76.4 all-gather.2
  216.4 109.8 reduce-scatter.2
  330.7 60.9 reduce-scatter.4
where the time goes:
time: 432 us; the launch traced here: 424 us
  waiting for transfers between devices  165 us (38%)
  Pallas kernels  85.6 us (20%)
  starting transfers between devices  48.6 us (11%)
  local copies, waits for them, and re-layouts  37.4 us (9%)
  other arithmetic  35.7 us (8%)
  matrix products  34.4 us (8%)
  between operations  16.9 us (4%)
    ppermute x35, waiting for transfers between devices, flip(): return lax.ppermute(value, axis, [(i, i ^ mask) for i in range(size)])  104 us
    all_to_all x2, waiting for transfers between devices, exchange(): lax.all_to_all(blocks, 'seq', 0, 0, axis_index_groups=teams, tiled=True)  47.9 us
    pallas_call x1, Pallas kernels, attend_backward(): pl.pallas_call(partial(bwd_body, nk=nk), grid_spec=pltpu.PrefetchScalarGr...  43.9 us
    ppermute x35, starting transfers between devices, flip(): return lax.ppermute(value, axis, [(i, i ^ mask) for i in range(size)])  39.7 us
    pallas_call x1, Pallas kernels, attend_forward(): pl.pallas_call(partial(fwd_body, bq=bq), grid=(n // bq, NH), in_specs=[pl...  28.3 us
    dot_general x4, matrix products, dot(): return jnp.dot(left, right, preferred_element_type=jnp.float32)  20.6 us
    reduce_scatter x2, waiting for transfers between devices, over_chips(): lax.psum_scatter(blocks, 'seq', scatter_dimension=0, tiled=False, axis_in...  12.6 us
    dot_general x4, matrix products, dot_t(): lax.dot_general(left, right, (((1,), (1,)), ((), ())), preferred_element_...  11.8 us
  transfers between devices with their start and end apart: 41, of which 24 were waited for; matrix products, arithmetic and copies ran while one was open for 16% of the time, Pallas kernels for 18%

commit v1 on v0

--- a/solution.py
+++ b/solution.py
@@ -452,10 +452,6 @@
         return blocks
 
     dinner = (dot_t(both_douter, outer_all) * slope).astype(bf16)
-    feed_blocks, dinner = lax.optimization_barrier(
-        (feed_grads(both_first, dinner, active, both_douter, chips), dinner)
-    )
-    feed_sums = over_chips(feed_blocks)
     dfirst_part = dot_t(dinner, inner_all)
     dfirst = dhidden_two + dfirst_part[:n_own] + sflip(dfirst_part[n_own:].astype(bf16), 1).astype(jnp.float32)
     dhidden_one, dfirst_gain, dfirst_shift = norm_back_one(dfirst)
@@ -471,14 +467,22 @@
     both_dattend = jnp.concatenate([dattend, sflip(dattend, 1)], axis=0)
     vectors = jnp.stack([dfirst_gain, dfirst_shift, dsecond_gain, dsecond_shift])
     other_blocks = other_grads(dinner, both_ctx, both_dattend, douter, vectors, chips)
-    other_blocks, dcontext = lax.optimization_barrier((other_blocks, dcontext))
+    feed_blocks = feed_grads(both_first, dinner, active, both_douter, chips)
+    feed_blocks, other_blocks, dcontext = lax.optimization_barrier((feed_blocks, other_blocks, dcontext))
+    feed_sums = over_chips(feed_blocks)
+
+    def halve(low, high, bit, mask):
+        sent = jnp.where(bit == 0, high, low).astype(bf16)
+        return jnp.where(bit == 0, low, high) + sflip(sent, mask).astype(jnp.float32)
+
+    def halve_other(blocks, b):
+        pairs = blocks.reshape((-1, 2) + blocks.shape[1:])
+        return halve(pairs[:, 0], pairs[:, 1], (me >> (b + 1)) % 2, 2 << b)
 
     last = part_bits[-1]
     dqueries, sent, kept = attend_backward(
         queries, kv, key_tail, context_full, stats, dcontext, ((me // last) % 2).astype(jnp.int32).reshape(1)
     )
-    sent, feed_sums, other_blocks = lax.optimization_barrier((sent, feed_sums, other_blocks))
-    other_sums = over_chips(other_blocks)
     dkv = (kept + sflip(sent, last).astype(jnp.float32)).reshape(n_parts // 2, 8 * rows, 2 * GROUP_WIDTH)
     for b in reversed(part_bits[:-1]):
         bit = (me // b) % 2
@@ -487,25 +491,24 @@
         sent = jnp.where(bit == 0, high, low).astype(bf16)
         dkv = jnp.where(bit == 0, low, high) + sflip(sent, b).astype(jnp.float32)
     dqkv = jnp.concatenate([dqueries, dkv[0].astype(bf16)], axis=1)
+    other_sums = halve_other(other_blocks, 0)
 
     dx = dot_t(dqkv, w_all).reshape(2, 2, 2, rows, width)
     da, db = dx[..., :half_width], dx[..., half_width:]
 
-    def halve(low, high, bit, mask):
-        sent = jnp.where(bit == 0, high, low).astype(bf16)
-        return jnp.where(bit == 0, low, high) + sflip(sent, mask).astype(jnp.float32)
-
     da = halve(da[:, :, 0], da[:, :, 1], y0, YO)
     db = halve(db[:, 0], db[:, 1], z0, ZO)
+    da, db, other_sums = lax.optimization_barrier((da, db, halve_other(other_sums, 1)))
     da = halve(da[:, 0], da[:, 1], z0, ZO)
     db = halve(db[:, 0], db[:, 1], y0, YO)
     dx = jnp.concatenate([da, db], axis=-1)
-    dx, other_sums = lax.optimization_barrier((dx, other_sums))
     mine = pick(dx, z1)
     theirs = sflip(pick(dx, 1 - z1).astype(bf16), HI).astype(jnp.float32)
     dtokens = dhidden_one.reshape(2, rows, width) + in_order(mine, theirs, z1)
 
-    feed_sums, other_sums = over_groups(feed_sums), over_groups(other_sums)
+    for b in range(2, log2_of(chips)):
+        other_sums = halve_other(other_sums, b)
+    feed_sums, other_sums = over_groups(feed_sums), over_groups(other_sums[0].astype(bf16))
     r1 = 4 * out_rows
     inner_grad = feed_sums[:r1].reshape(2, 2, out_rows, width)
     inner_grad = [inner_grad[:, i] for i in range(2)]

time: 432 us -> 424 us (0.981)
  waiting for transfers between devices: 165 us -> 141 us
  other arithmetic: 35.7 us -> 44.6 us
  local copies, waits for them, and re-layouts: 37.4 us -> 43.3 us
    all_to_all x2, waiting for transfers between devices: 47.9 us -> 19.7 us  [exchange(): lax.all_to_all(blocks, 'seq', 0, 0, axis_index_groups=teams, tiled=True)]
    ppermute x35 -> x38, waiting for transfers between devices: 104 us -> 122 us  [flip(): return lax.ppermute(value, axis, [(i, i ^ mask) for i in range(size)])]
    reduce_scatter x2 -> x1, waiting for transfers between devices: 12.6 us -> 0.01 us  [over_chips(): lax.psum_scatter(blocks, 'seq', scatter_dimension=0, tiled=False, axis_in...]
    dot_general x4, matrix products: 20.6 us -> 28.4 us  [dot(): return jnp.dot(left, right, preferred_element_type=jnp.float32)]
    ppermute x35 -> x38, starting transfers between devices: 39.7 us -> 39.1 us  [flip(): return lax.ppermute(value, axis, [(i, i ^ mask) for i in range(size)])]
  transfers between devices with their start and end apart: 41 -> 43, of which waited for: 24 -> 21; matrix products, arithmetic and copies ran while one was open for 16% -> 18% of each run, Pallas kernels for 18% -> 20%
where the time goes in v1:
time: 424 us; the launch traced here: 419 us
  waiting for transfers between devices  141 us (33%)
  Pallas kernels  85.3 us (20%)
  starting transfers between devices  48.5 us (11%)
  other arithmetic  44.6 us (11%)
  local copies, waits for them, and re-layouts  43.3 us (10%)
  matrix products  38.7 us (9%)
  between operations  17.1 us (4%)
    ppermute x38, waiting for transfers between devices, flip(): return lax.ppermute(value, axis, [(i, i ^ mask) for i in range(size)])  122 us
    pallas_call x1, Pallas kernels, attend_backward(): pl.pallas_call(partial(bwd_body, nk=nk), grid_spec=pltpu.PrefetchScalarGr...  43.6 us
    ppermute x38, starting transfers between devices, flip(): return lax.ppermute(value, axis, [(i, i ^ mask) for i in range(size)])  39.1 us
    pallas_call x1, Pallas kernels, attend_forward(): pl.pallas_call(partial(fwd_body, bq=bq), grid=(n // bq, NH), in_specs=[pl...  28.4 us
    dot_general x4, matrix products, dot(): return jnp.dot(left, right, preferred_element_type=jnp.float32)  28.4 us
    all_to_all x2, waiting for transfers between devices, exchange(): lax.all_to_all(blocks, 'seq', 0, 0, axis_index_groups=teams, tiled=True)  19.7 us
    pallas_call x1, Pallas kernels, feed_grads(): pl.pallas_call(partial(feed_grads_body, chips=chips), out_shape=jax.Shape...  9.07 us
  transfers between devices with their start and end apart: 43, of which 21 were waited for; matrix products, arithmetic and copies ran while one was open for 18% of the time, Pallas kernels for 20%

profile of v1, /device:TPU:0, one launch (start us, length us, event | category | flops | bytes accessed | tf_op | source)
XLA Modules:
  0.0 418.7 jit_solution(16152096716688941812)
XLA Ops:
  7.3 1.7 collective-permute-start.13
  10.8 3.5 collective-permute-start.12
  14.4 2.7 collective-permute-start
  22.1 8.5 %collective-permute-done = bf16[192,768]{1,0:T(8,128)(2,1)S(1)} collective-permute-done((bf16[192,768]{1,0:T(8,128)(2,1)S(1)}, bf16[192,768]{1,0:T(8,128)(2,1)S(1)}, u32[]{:S(2)}, u32[]{:S(2)}) %collective-permute-start) | collective-permute-done | bytes 294944 | tf_op jit(solution)/shard_map/ppermute | solution.py:28
  31.2 1.6 collective-permute-start.6
  34.5 2.1 collective-permute-start.3
  37.9 2.4 collective-permute-done.6
  40.3 1.6 collective-permute-start.8
  42.1 10.6 %collective-permute-done.8 = bf16[2,2,32,576]{3,2,1,0:T(8,128)(2,1)S(1)} collective-permute-done((bf16[2,2,32,576]{3,2,1,0:T(8,128)(2,1)S(1)}, bf16[2,2,32,576]{3,2,1,0:T(8,128)(2,1)S(1)}, u32[]{:S(2)}, u32[]{:S(2)}) %collective-permute-start.8) | collective-permute-done | bytes 147488 | tf_op jit(solution)/shard_map/ppermute | solution.py:28
  52.8 1.7 collective-permute-start.9
  54.8 4.4 %collective-permute-start.2 = (bf16[2,2,192,384]{3,2,1,0:T(8,128)(2,1)S(1)}, bf16[2,2,192,384]{3,2,1,0:T(8,128)(2,1)S(1)}, u32[]{:S(2)}, u32[]{:S(2)}) collective-permute-start(bf16[2,2,192,384]{3,2,1,0:T(8,128)(2,1)S(1)} %maximum_select_fusion.12), channel_id=1, source_target_pairs={{0,4},{1,5},{2,6},{3,7},{4,0},{5,1},{6,2},{7,3},{8,12},{9,13},{10,... | collective-permute-start | bytes 1769480 | tf_op jit(solution)/shard_map/ppermute | solution.py:28
  62.3 24.4 %collective-permute-done.2 = bf16[2,2,192,384]{3,2,1,0:T(8,128)(2,1)S(1)} collective-permute-done((bf16[2,2,192,384]{3,2,1,0:T(8,128)(2,1)S(1)}, bf16[2,2,192,384]{3,2,1,0:T(8,128)(2,1)S(1)}, u32[]{:S(2)}, u32[]{:S(2)}) %collective-permute-start.2) | collective-permute-done | bytes 589856 | tf_op jit(solution)/shard_map/ppermute | solution.py:28
  92.3 3.2 convolution_add_fusion
  98.9 1.8 maximum_select_fusion
  101.2 28.4 %attend_forward.1 = (bf16[1536,192]{1,0:T(8,128)(2,1)}, f32[1536,192]{1,0:T(8,128)}, f32[1536,128]{1,0:T(8,128)}) custom-call(bf16[1536,192]{1,0:T(8,128)(2,1)} %fusion.8.q_ref, bf16[3072,384]{1,0:T(8,128)(2,1)} %bitcast.358, bf16[3072,128]{1,0:T(8,128)(2,1)} %select_convert_fusion.kb_ref), custom_call_target="tpu_custom_call" | custom-call | flops 14495514624 | bytes 18874368 | tf_op jit(solution)/shard_map/attend_forward/pallas_call | solution.py:103
  129.6 3.5 all-to-all-start
  134.4 19.1 %all-to-all-done = bf16[8,192,192]{2,1,0:T(8,128)(2,1)S(1)} async-done(((bf16[8,192,192]{2,1,0:T(8,128)(2,1)}), bf16[8,192,192]{2,1,0:T(8,128)(2,1)S(1)}, u32[]{:S(2)}, u32[]{:S(2)}) %all-to-all-start) | async-done | bytes 589856 | tf_op jit(solution)/shard_map/all_to_all | solution.py:410
  154.8 1.5 slice_bitcast_fusion.7
  157.7 9.2 %collective-permute-done.14 = bf16[8,240,768]{2,1,0:T(8,128)(2,1)} collective-permute-done((bf16[8,240,768]{2,1,0:T(8,128)(2,1)}, bf16[8,240,768]{2,1,0:T(8,128)(2,1)}, u32[]{:S(2)}, u32[]{:S(2)}) %collective-permute-start.14) | collective-permute-done | bytes 2949152 | tf_op jit(solution)/shard_map/ppermute | solution.py:28
  172.6 22.4 %multiply_convert_fusion.1 = (bf16[768,1536]{1,0:T(8,128)(2,1)S(1)}, f32[768,1536]{1,0:T(8,128)}, f32[768,1536]{1,0:T(8,128)}) fusion(f32[1536]{0:T(1024)S(1)} %select_n.868, bf16[768,768]{1,0:T(8,128)(2,1)S(1)} %bitcast.391, bf16[768,768]{1,0:T(8,128)(2,1)S(1)} %bitcast.389, bf16[384,768]{1,0:T(8,128)(2,1)S(1)} %collective-permute-done.15, ...), kind=kOutput, calls=%fused_computation.3 | convolution fusion | flops 1896873984 | bytes 15341568 | tf_op jit(solution)/shard_map/dot_general | solution.py:46
  195.1 2.0 fusion.80
  200.7 1.9 fusion.70
  206.2 1.6 collective-permute-done.17
  207.9 3.5 multiply_convert_fusion.dz_ref
  211.5 2.0 fusion.9
  216.7 1.9 copy.131
  218.6 2.4 reshape_reshape.2
  223.1 1.9 copy.132
  225.1 2.2 multiply_reduce_fusion
  231.8 3.7 all-to-all-start.1
  236.0 1.8 pad_maximum_fusion.10.ctx_ref
  240.6 9.1 %feed_grads.1 = bf16[8,384,768]{2,1,0:T(8,128)(2,1)} custom-call(bf16[768,768]{1,0:T(8,128)(2,1)} %pad_maximum_fusion.6.y_ref, bf16[768,1536]{1,0:T(8,128)(2,1)} %copy-done.11, bf16[768,1536]{1,0:T(8,128)(2,1)} %copy-done.46, bf16[768,768]{1,0:T(8,128)(2,1)} %pad_maximum_fusion.7.do_ref), custom_call_target="tpu_custom_call" | custom-call | flops 3623878656 | bytes 11796480 | tf_op jit(solution)/shard_map/feed_grads/pallas_call | solution.py:206
  251.4 4.3 %other_grads.1 = bf16[8,56,768]{2,1,0:T(8,128)(2,1)} custom-call(bf16[768,1536]{1,0:T(8,128)(2,1)} %copy-done.11, bf16[768,384]{1,0:T(8,128)(2,1)} %pad_maximum_fusion.10.ctx_ref, bf16[768,768]{1,0:T(8,128)(2,1)} %pad_maximum_fusion.8.da_ref, bf16[384,768]{1,0:T(8,128)(2,1)} %copy-done.3, f32[4,768]{1,0:T(4,128)} %pad_maximum_fusion.15.vec_ref), custom_call_target="tpu_custom_call" | custom-call | flops 452984832 | bytes 5898240 | tf_op jit(solution)/shard_map/other_grads/pallas_call | solution.py:232
  259.3 43.6 %attend_backward.1 = (bf16[1536,192]{1,0:T(8,128)(2,1)}, bf16[1536,384]{1,0:T(8,128)(2,1)}, f32[1536,384]{1,0:T(8,128)}) custom-call(s32[1]{0:T(128)} %bitcast.73.bit_ref, bf16[1536,192]{1,0:T(8,128)(2,1)} %fusion.8.q_ref, bf16[3072,384]{1,0:T(8,128)(2,1)} %bitcast.359, bf16[3072,128]{1,0:T(8,128)(2,1)} %select_convert_fusion.kb_ref, ...), custom_call_target="tpu_custom_call" | custom-call | tf_op jit(solution)/shard_map/attend_backward/pallas_call | solution.py:176
  306.2 2.6 copy.152
  308.9 2.9 collective-permute-done.25
  311.8 2.4 add_convert_fusion
  315.3 2.1 fusion.6
  318.9 2.0 fusion.81
  324.3 2.4 collective-permute-start.30
  326.6 35.1 %collective-permute-done.23 = bf16[2,2,192,384]{3,2,1,0:T(8,128)(2,1)S(1)} collective-permute-done((bf16[2,2,192,384]{3,2,1,0:T(8,128)(2,1)S(1)}, bf16[2,2,192,384]{3,2,1,0:T(8,128)(2,1)S(1)}, u32[]{:S(2)}, u32[]{:S(2)}) %collective-permute-start.23) | collective-permute-done | bytes 589856 | tf_op jit(solution)/shard_map/ppermute | solution.py:28
  364.2 4.3 %collective-permute-done.35 = bf16[1,56,768]{2,1,0:T(8,128)(2,1)S(1)} collective-permute-done((bf16[1,56,768]{2,1,0:T(8,128)(2,1)S(1)}, bf16[1,56,768]{2,1,0:T(8,128)(2,1)S(1)}, u32[]{:S(2)}, u32[]{:S(2)}) %collective-permute-start.35) | collective-permute-done | bytes 86048 | tf_op jit(solution)/shard_map/ppermute | solution.py:28
  370.3 2.8 collective-permute-done.36
  380.6 2.9 collective-permute-done.31
  385.1 3.2 collective-permute-start.32
  388.3 4.2 %collective-permute-done.34 = bf16[56,576]{1,0:T(8,128)(2,1)S(1)} collective-permute-done((bf16[56,576]{1,0:T(8,128)(2,1)S(1)}, bf16[56,576]{1,0:T(8,128)(2,1)S(1)}, u32[]{:S(2)}, u32[]{:S(2)}) %collective-permute-start.34) | collective-permute-done | bytes 64544 | tf_op jit(solution)/shard_map/ppermute | solution.py:28
  396.7 8.0 %collective-permute-done.37 = bf16[384,768]{1,0:T(8,128)(2,1)S(1)} collective-permute-done((bf16[384,768]{1,0:T(8,128)(2,1)}, bf16[384,768]{1,0:T(8,128)(2,1)S(1)}, u32[]{:S(2)}, u32[]{:S(2)}) %collective-permute-start.37) | collective-permute-done | bytes 589856 | tf_op jit(solution)/shard_map/ppermute | solution.py:28
  410.1 1.6 reshape.1459
  (344 shorter events, 88.8 us)
Async XLA Ops:
  7.2 93.4 %all-gather.3.cloned.1.call-start = ((), (), s32[]{:S(2)}) async-start(), calls=%async_computation.4 | async-start | bytes 3317760 | tf_op jit(solution)/shard_map/all_gather | solution.py:321
  7.3 14.0 %collective-permute-start.13 = (bf16[96,768]{1,0:T(8,128)(2,1)}, bf16[96,768]{1,0:T(8,128)(2,1)S(1)}, u32[]{:S(2)}, u32[]{:S(2)}) collective-permute-start(bf16[96,768]{1,0:T(8,128)(2,1)} %param.33), channel_id=1, source_target_pairs={{0,0},{1,2},{2,1},{3,3},{4,4},{5,6},{6,5},{7,7},{8,8},{9,10},{10,9... | collective-permute-start | bytes 442376 | tf_op jit(solution)/shard_map/ppermute | solution.py:306
  10.8 10.1 %collective-permute-start.12 = (bf16[72,768]{1,0:T(8,128)(2,1)S(1)}, bf16[72,768]{1,0:T(8,128)(2,1)S(1)}, u32[]{:S(2)}, u32[]{:S(2)}) collective-permute-start(bf16[72,768]{1,0:T(8,128)(2,1)S(1)} %pad_maximum_fusion.14), channel_id=1, source_target_pairs={{0,1},{1,0},{2,3},{3,2},{4,5},{5,4},{6,7},{7,6},{8,9},{9,8},{10,11... | collective-permute-start | bytes 331784 | tf_op jit(solution)/shard_map/ppermute | solution.py:28
  14.4 16.2 %collective-permute-start = (bf16[192,768]{1,0:T(8,128)(2,1)S(1)}, bf16[192,768]{1,0:T(8,128)(2,1)S(1)}, u32[]{:S(2)}, u32[]{:S(2)}) collective-permute-start(bf16[192,768]{1,0:T(8,128)(2,1)S(1)} %get-tuple-element.91), channel_id=1, source_target_pairs={{0,8},{1,9},{2,10},{3,11},{4,12},{5,13},{6,14},{7,15},{8,0},{9,1},... | collective-permute-start | bytes 884744 | tf_op jit(solution)/shard_map/ppermute | solution.py:28
  30.6 7.3 %collective-permute-start.7 = (bf16[32,576]{1,0:T(8,128)(2,1)S(1)}, bf16[32,576]{1,0:T(8,128)(2,1)S(1)}, u32[]{:S(2)}, u32[]{:S(2)}) collective-permute-start(bf16[32,576]{1,0:T(8,128)(2,1)S(1)} %get-tuple-element.118), channel_id=1, source_target_pairs={{0,6},{1,7},{2,4},{3,5},{4,2},{5,3},{6,0},{7,1},{8,14},{9,15},{10,... | collective-permute-start | bytes 110600 | tf_op jit(solution)/shard_map/ppermute | solution.py:28
  31.2 9.1 %collective-permute-start.6 = (bf16[32,576]{1,0:T(8,128)(2,1)S(1)}, bf16[32,576]{1,0:T(8,128)(2,1)S(1)}, u32[]{:S(2)}, u32[]{:S(2)}) collective-permute-start(bf16[32,576]{1,0:T(8,128)(2,1)S(1)} %get-tuple-element.119), channel_id=1, source_target_pairs={{0,4},{1,5},{2,6},{3,7},{4,0},{5,1},{6,2},{7,3},{8,12},{9,13},{10,... | collective-permute-start | bytes 110600 | tf_op jit(solution)/shard_map/ppermute | solution.py:28
  32.8 4.2 %collective-permute-start.5 = (bf16[32,576]{1,0:T(8,128)(2,1)S(1)}, bf16[32,576]{1,0:T(8,128)(2,1)S(1)}, u32[]{:S(2)}, u32[]{:S(2)}) collective-permute-start(bf16[32,576]{1,0:T(8,128)(2,1)S(1)} %get-tuple-element.120), channel_id=1, source_target_pairs={{0,2},{1,3},{2,0},{3,1},{4,6},{5,7},{6,4},{7,5},{8,10},{9,11},{10,... | collective-permute-start | bytes 110600 | tf_op jit(solution)/shard_map/ppermute | solution.py:28
  34.5 24.7 %collective-permute-start.3 = (bf16[2,192,384]{2,1,0:T(8,128)(2,1)S(1)}, bf16[2,192,384]{2,1,0:T(8,128)(2,1)S(1)}, u32[]{:S(2)}, u32[]{:S(2)}) collective-permute-start(bf16[2,192,384]{2,1,0:T(8,128)(2,1)S(1)} %get-tuple-element.88), channel_id=1, source_target_pairs={{0,4},{1,5},{2,6},{3,7},{4,0},{5,1},{6,2},{7,3},{8,12},{9,13},{10,... | collective-permute-start | bytes 884744 | tf_op jit(solution)/shard_map/ppermute | solution.py:28
  36.6 18.1 %collective-permute-start.1 = (bf16[2,192,384]{2,1,0:T(8,128)(2,1)S(1)}, bf16[2,192,384]{2,1,0:T(8,128)(2,1)S(1)}, u32[]{:S(2)}, u32[]{:S(2)}) collective-permute-start(bf16[2,192,384]{2,1,0:T(8,128)(2,1)S(1)} %get-tuple-element.89), channel_id=1, source_target_pairs={{0,2},{1,3},{2,0},{3,1},{4,6},{5,7},{6,4},{7,5},{8,10},{9,11},{10,... | collective-permute-start | bytes 884744 | tf_op jit(solution)/shard_map/ppermute | solution.py:28
  40.3 12.3 %collective-permute-start.8 = (bf16[2,2,32,576]{3,2,1,0:T(8,128)(2,1)S(1)}, bf16[2,2,32,576]{3,2,1,0:T(8,128)(2,1)S(1)}, u32[]{:S(2)}, u32[]{:S(2)}) collective-permute-start(bf16[2,2,32,576]{3,2,1,0:T(8,128)(2,1)S(1)} %maximum_select_fusion.19), channel_id=1, source_target_pairs={{0,8},{1,9},{2,10},{3,11},{4,12},{5,13},{6,14},{7,15},{8,0},{9,1},... | collective-permute-start | bytes 442376 | tf_op jit(solution)/shard_map/ppermute | solution.py:28
  52.8 9.0 %collective-permute-start.9 = (bf16[2,2,2,32,576]{4,3,2,1,0:T(8,128)(2,1)S(1)}, bf16[2,2,2,32,576]{4,3,2,1,0:T(8,128)(2,1)S(1)}, u32[]{:S(2)}, u32[]{:S(2)}) collective-permute-start(bf16[2,2,2,32,576]{4,3,2,1,0:T(8,128)(2,1)S(1)} %maximum_select_fusion.16), channel_id=1, source_target_pairs={{0,16},{16,0},{1,17},{17,1},{2,18},{18,2},{3,19},{19,3},{4,20},{20... | collective-permute-start | bytes 884744 | tf_op jit(solution)/shard_map/ppermute | solution.py:28
  54.8 31.9 %collective-permute-start.2 = (bf16[2,2,192,384]{3,2,1,0:T(8,128)(2,1)S(1)}, bf16[2,2,192,384]{3,2,1,0:T(8,128)(2,1)S(1)}, u32[]{:S(2)}, u32[]{:S(2)}) collective-permute-start(bf16[2,2,192,384]{3,2,1,0:T(8,128)(2,1)S(1)} %maximum_select_fusion.12), channel_id=1, source_target_pairs={{0,4},{1,5},{2,6},{3,7},{4,0},{5,1},{6,2},{7,3},{8,12},{9,13},{10,... | collective-permute-start | bytes 1769480 | tf_op jit(solution)/shard_map/ppermute | solution.py:28
  59.3 28.3 %collective-permute-start.4 = (bf16[2,2,192,384]{3,2,1,0:T(8,128)(2,1)S(1)}, bf16[2,2,192,384]{3,2,1,0:T(8,128)(2,1)S(1)}, u32[]{:S(2)}, u32[]{:S(2)}) collective-permute-start(bf16[2,2,192,384]{3,2,1,0:T(8,128)(2,1)S(1)} %maximum_select_fusion.14), channel_id=1, source_target_pairs={{0,2},{1,3},{2,0},{3,1},{4,6},{5,7},{6,4},{7,5},{8,10},{9,11},{10,... | collective-permute-start | bytes 1769480 | tf_op jit(solution)/shard_map/ppermute | solution.py:28
  61.9 26.2 %collective-permute-start.10 = (bf16[2,2,2,2,32,576]{5,4,3,2,1,0:T(8,128)(2,1)S(1)}, bf16[2,2,2,2,32,576]{5,4,3,2,1,0:T(8,128)(2,1)S(1)}, u32[]{:S(2)}, u32[]{:S(2)}) collective-permute-start(bf16[2,2,2,2,32,576]{5,4,3,2,1,0:T(8,128)(2,1)S(1)} %maximum_select_fusion.10), channel_id=1, source_target_pairs={{0,1},{1,0},{2,3},{3,2},{4,5},{5,4},{6,7},{7,6},{8,9},{9,8},{10,11... | collective-permute-start | bytes 1769480 | tf_op jit(solution)/shard_map/ppermute | solution.py:28
  95.9 2.9 collective-permute-start.11
  100.6 66.2 %collective-permute-start.14 = (bf16[8,240,768]{2,1,0:T(8,128)(2,1)}, bf16[8,240,768]{2,1,0:T(8,128)(2,1)}, u32[]{:S(2)}, u32[]{:S(2)}) collective-permute-start(bf16[8,240,768]{2,1,0:T(8,128)(2,1)} %bitcast.375), channel_id=1, source_target_pairs={{0,16},{16,0},{1,17},{17,1},{2,18},{18,2},{3,19},{19,3},{4,20},{20... | collective-permute-start | bytes 8847368 | tf_op jit(solution)/shard_map/ppermute | solution.py:28
  129.6 23.9 %all-to-all-start = ((bf16[8,192,192]{2,1,0:T(8,128)(2,1)}), bf16[8,192,192]{2,1,0:T(8,128)(2,1)S(1)}, u32[]{:S(2)}, u32[]{:S(2)}) async-start(bf16[8,192,192]{2,1,0:T(8,128)(2,1)} %bitcast.405), calls=%async_computation | async-start | bytes 1572864 | tf_op jit(solution)/shard_map/all_to_all | solution.py:410
  170.2 2.4 collective-permute-start.15
  172.2 22.9 %copy-start.12 = (bf16[2,8,96,768]{3,2,1,0:T(8,128)(2,1)}, bf16[2,8,96,768]{3,2,1,0:T(8,128)(2,1)S(1)}, u32[]{:S(2)}) copy-start(bf16[2,8,96,768]{3,2,1,0:T(8,128)(2,1)S(1)} %maximum_select_fusion.1) | copy-start | bytes 7077892
  172.6 22.5 %copy-start.19 = (bf16[2,8,48,768]{3,2,1,0:T(8,128)(2,1)}, bf16[2,8,48,768]{3,2,1,0:T(8,128)(2,1)S(1)}, u32[]{:S(2)}) copy-start(bf16[2,8,48,768]{3,2,1,0:T(8,128)(2,1)S(1)} %get-tuple-element.134) | copy-start | bytes 3538948
  172.6 22.5 %copy-start.21 = (bf16[2,8,48,768]{3,2,1,0:T(8,128)(2,1)}, bf16[2,8,48,768]{3,2,1,0:T(8,128)(2,1)S(1)}, u32[]{:S(2)}) copy-start(bf16[2,8,48,768]{3,2,1,0:T(8,128)(2,1)S(1)} %get-tuple-element.135) | copy-start | bytes 3538948
  172.6 22.5 %copy-start.28 = (bf16[384,768]{1,0:T(8,128)(2,1)}, bf16[384,768]{1,0:T(8,128)(2,1)S(1)}, u32[]{:S(2)}) copy-start(bf16[384,768]{1,0:T(8,128)(2,1)S(1)} %collective-permute-done.15) | copy-start | bytes 1769476
  198.6 2.1 collective-permute-start.16
  205.8 2.1 collective-permute-start.17
  215.2 10.0 %collective-permute-start.18 = (bf16[384,768]{1,0:T(8,128)(2,1)}, bf16[384,768]{1,0:T(8,128)(2,1)}, u32[]{:S(2)}, u32[]{:S(2)}) collective-permute-start(bf16[384,768]{1,0:T(8,128)(2,1)} %slice.573), channel_id=1, source_target_pairs={{0,1},{1,0},{2,3},{3,2},{4,5},{5,4},{6,7},{7,6},{8,9},{9,8},{10,11... | collective-permute-start | bytes 1769480 | tf_op jit(solution)/shard_map/ppermute | solution.py:28
  225.0 11.0 %collective-permute-start.19 = (bf16[384,384]{1,0:T(8,128)(2,1)}, bf16[384,384]{1,0:T(8,128)(2,1)}, u32[]{:S(2)}, u32[]{:S(2)}) collective-permute-start(bf16[384,384]{1,0:T(8,128)(2,1)} %copy.132), channel_id=1, source_target_pairs={{0,1},{1,0},{2,3},{3,2},{4,5},{5,4},{6,7},{7,6},{8,9},{9,8},{10,11... | collective-permute-start | bytes 884744 | tf_op jit(solution)/shard_map/ppermute | solution.py:28
  231.8 24.5 %all-to-all-start.1 = ((bf16[8,192,192]{2,1,0:T(8,128)(2,1)}), bf16[8,192,192]{2,1,0:T(8,128)(2,1)S(1)}, u32[]{:S(2)}, u32[]{:S(2)}) async-start(bf16[8,192,192]{2,1,0:T(8,128)(2,1)} %bitcast.78), calls=%async_computation.1 | async-start | bytes 1572864 | tf_op jit(solution)/shard_map/all_to_all | solution.py:410
  235.5 159.2 %reduce-scatter.2.cloned.1.call-start = ((), (), s32[]{:S(2)}) async-start(), calls=%async_computation.3 | async-start | bytes 5308416 | tf_op jit(solution)/shard_map/reduce_scatter | solution.py:447
  239.0 11.3 %collective-permute-start.20 = (bf16[384,768]{1,0:T(8,128)(2,1)S(1)}, bf16[384,768]{1,0:T(8,128)(2,1)S(1)}, u32[]{:S(2)}, u32[]{:S(2)}) collective-permute-start(bf16[384,768]{1,0:T(8,128)(2,1)S(1)} %get-tuple-element.60), channel_id=1, source_target_pairs={{0,1},{1,0},{2,3},{3,2},{4,5},{5,4},{6,7},{7,6},{8,9},{9,8},{10,11... | collective-permute-start | bytes 1769480 | tf_op jit(solution)/shard_map/ppermute | solution.py:28
  257.8 45.1 %collective-permute-start.24 = (bf16[4,56,768]{2,1,0:T(8,128)(2,1)S(1)}, bf16[4,56,768]{2,1,0:T(8,128)(2,1)}, u32[]{:S(2)}, u32[]{:S(2)}) collective-permute-start(bf16[4,56,768]{2,1,0:T(8,128)(2,1)S(1)} %select_bitcast_fusion), channel_id=1, source_target_pairs={{0,2},{1,3},{2,0},{3,1},{4,6},{5,7},{6,4},{7,5},{8,10},{9,11},{10,... | collective-permute-start | bytes 1032200 | tf_op jit(solution)/shard_map/ppermute | solution.py:28
  259.3 47.0 %copy-start.1 = (bf16[2,2,2,192,768]{4,3,2,1,0:T(8,128)(2,1)S(1)}, bf16[2,2,2,192,768]{4,3,2,1,0:T(8,128)(2,1)}, u32[]{:S(2)}) copy-start(bf16[2,2,2,192,768]{4,3,2,1,0:T(8,128)(2,1)} %copy-done) | copy-start | bytes 7077892
  302.8 9.0 %collective-permute-start.21 = (bf16[1536,384]{1,0:T(8,128)(2,1)}, bf16[1536,384]{1,0:T(8,128)(2,1)}, u32[]{:S(2)}, u32[]{:S(2)}) collective-permute-start(bf16[1536,384]{1,0:T(8,128)(2,1)} %get-tuple-element.49), channel_id=1, source_target_pairs={{0,1},{1,0},{2,3},{3,2},{4,5},{5,4},{6,7},{7,6},{8,9},{9,8},{10,11... | collective-permute-start | bytes 3538952 | tf_op jit(solution)/shard_map/ppermute | solution.py:28
  304.9 6.8 %collective-permute-start.25 = (bf16[2,56,768]{2,1,0:T(8,128)(2,1)S(1)}, bf16[2,56,768]{2,1,0:T(8,128)(2,1)S(1)}, u32[]{:S(2)}, u32[]{:S(2)}) collective-permute-start(bf16[2,56,768]{2,1,0:T(8,128)(2,1)S(1)} %fusion.43), channel_id=1, source_target_pairs={{0,4},{1,5},{2,6},{3,7},{4,0},{5,1},{6,2},{7,3},{8,12},{9,13},{10,... | collective-permute-start | bytes 516104 | tf_op jit(solution)/shard_map/ppermute | solution.py:28
  317.7 5.7 %collective-permute-start.29 = (bf16[2,2,1,2,56,576]{5,4,3,1,0,2:T(8,128)(2,1)S(1)}, bf16[2,2,1,2,56,576]{5,4,3,1,0,2:T(8,128)(2,1)S(1)}, u32[]{:S(2)}, u32[]{:S(2)}) collective-permute-start(bf16[2,2,1,2,56,576]{5,4,3,1,0,2:T(8,128)(2,1)S(1)} %fusion.34), channel_id=1, source_target_pairs={{0,1},{1,0},{2,3},{3,2},{4,5},{5,4},{6,7},{7,6},{8,9},{9,8},{10,11... | collective-permute-start | bytes 1548296 | tf_op jit(solution)/shard_map/ppermute | solution.py:28
  321.1 40.7 %collective-permute-start.23 = (bf16[2,2,192,384]{3,2,1,0:T(8,128)(2,1)S(1)}, bf16[2,2,192,384]{3,2,1,0:T(8,128)(2,1)S(1)}, u32[]{:S(2)}, u32[]{:S(2)}) collective-permute-start(bf16[2,2,192,384]{3,2,1,0:T(8,128)(2,1)S(1)} %fusion.30), channel_id=1, source_target_pairs={{0,4},{1,5},{2,6},{3,7},{4,0},{5,1},{6,2},{7,3},{8,12},{9,13},{10,... | collective-permute-start | bytes 1769480 | tf_op jit(solution)/shard_map/ppermute | solution.py:28
  322.7 39.3 %collective-permute-start.22 = (bf16[2,2,192,384]{3,2,0,1:T(8,128)(2,1)S(1)}, bf16[2,2,192,384]{3,2,0,1:T(8,128)(2,1)S(1)}, u32[]{:S(2)}, u32[]{:S(2)}) collective-permute-start(bf16[2,2,192,384]{3,2,0,1:T(8,128)(2,1)S(1)} %fusion.29), channel_id=1, source_target_pairs={{0,2},{1,3},{2,0},{3,1},{4,6},{5,7},{6,4},{7,5},{8,10},{9,11},{10,... | collective-permute-start | bytes 1769480 | tf_op jit(solution)/shard_map/ppermute | solution.py:28
  324.3 51.5 %collective-permute-start.30 = (bf16[2,2,56,576]{3,2,1,0:T(8,128)(2,1)}, bf16[2,2,56,576]{3,2,1,0:T(8,128)(2,1)}, u32[]{:S(2)}, u32[]{:S(2)}) collective-permute-start(bf16[2,2,56,576]{3,2,1,0:T(8,128)(2,1)} %fusion.41), channel_id=1, source_target_pairs={{0,8},{1,9},{2,10},{3,11},{4,12},{5,13},{6,14},{7,15},{8,0},{9,1},... | collective-permute-start | bytes 774152 | tf_op jit(solution)/shard_map/ppermute | solution.py:28
  362.1 6.4 %collective-permute-start.35 = (bf16[1,56,768]{2,1,0:T(8,128)(2,1)S(1)}, bf16[1,56,768]{2,1,0:T(8,128)(2,1)S(1)}, u32[]{:S(2)}, u32[]{:S(2)}) collective-permute-start(bf16[1,56,768]{2,1,0:T(8,128)(2,1)S(1)} %fusion.47), channel_id=1, source_target_pairs={{0,8},{1,9},{2,10},{3,11},{4,12},{5,13},{6,14},{7,15},{8,0},{9,1},... | collective-permute-start | bytes 258056 | tf_op jit(solution)/shard_map/ppermute | solution.py:28
  368.5 4.6 %collective-permute-start.36 = (bf16[56,768]{1,0:T(8,128)(2,1)S(1)}, bf16[56,768]{1,0:T(8,128)(2,1)S(1)}, u32[]{:S(2)}, u32[]{:S(2)}) collective-permute-start(bf16[56,768]{1,0:T(8,128)(2,1)S(1)} %fusion.48), channel_id=1, source_target_pairs={{0,16},{16,0},{1,17},{17,1},{2,18},{18,2},{3,19},{19,3},{4,20},{20... | collective-permute-start | bytes 258056 | tf_op jit(solution)/shard_map/ppermute | solution.py:28
  369.9 7.5 %collective-permute-start.27 = (bf16[2,192,384]{2,1,0:T(8,128)(2,1)}, bf16[2,192,384]{2,1,0:T(8,128)(2,1)}, u32[]{:S(2)}, u32[]{:S(2)}) collective-permute-start(bf16[2,192,384]{2,1,0:T(8,128)(2,1)} %fusion.40), channel_id=1, source_target_pairs={{0,2},{1,3},{2,0},{3,1},{4,6},{5,7},{6,4},{7,5},{8,10},{9,11},{10,... | collective-permute-start | bytes 884744 | tf_op jit(solution)/shard_map/ppermute | solution.py:28
  369.9 8.5 %collective-permute-start.26 = (bf16[2,192,384]{2,1,0:T(8,128)(2,1)}, bf16[2,192,384]{2,1,0:T(8,128)(2,1)}, u32[]{:S(2)}, u32[]{:S(2)}) collective-permute-start(bf16[2,192,384]{2,1,0:T(8,128)(2,1)} %fusion.38), channel_id=1, source_target_pairs={{0,4},{1,5},{2,6},{3,7},{4,0},{5,1},{6,2},{7,3},{8,12},{9,13},{10,... | collective-permute-start | bytes 884744 | tf_op jit(solution)/shard_map/ppermute | solution.py:28
  376.8 6.7 %collective-permute-start.31 = (bf16[2,2,56,576]{3,2,1,0:T(8,128)(2,1)S(1)}, bf16[2,2,56,576]{3,2,1,0:T(8,128)(2,1)S(1)}, u32[]{:S(2)}, u32[]{:S(2)}) collective-permute-start(bf16[2,2,56,576]{3,2,1,0:T(8,128)(2,1)S(1)} %fusion.51), channel_id=1, source_target_pairs={{0,16},{16,0},{1,17},{17,1},{2,18},{18,2},{3,19},{19,3},{4,20},{20... | collective-permute-start | bytes 774152 | tf_op jit(solution)/shard_map/ppermute | solution.py:28
  379.6 17.1 %collective-permute-start.28 = (bf16[192,768]{1,0:T(8,128)(2,1)S(1)}, bf16[192,768]{1,0:T(8,128)(2,1)S(1)}, u32[]{:S(2)}, u32[]{:S(2)}) collective-permute-start(bf16[192,768]{1,0:T(8,128)(2,1)S(1)} %fusion.39), channel_id=1, source_target_pairs={{0,8},{1,9},{2,10},{3,11},{4,12},{5,13},{6,14},{7,15},{8,0},{9,1},... | collective-permute-start | bytes 884744 | tf_op jit(solution)/shard_map/ppermute | solution.py:28
  384.6 7.9 %collective-permute-start.34 = (bf16[56,576]{1,0:T(8,128)(2,1)S(1)}, bf16[56,576]{1,0:T(8,128)(2,1)S(1)}, u32[]{:S(2)}, u32[]{:S(2)}) collective-permute-start(bf16[56,576]{1,0:T(8,128)(2,1)S(1)} %get-tuple-element.112), channel_id=1, source_target_pairs={{0,6},{1,7},{2,4},{3,5},{4,2},{5,3},{6,0},{7,1},{8,14},{9,15},{10,... | collective-permute-start | bytes 193544 | tf_op jit(solution)/shard_map/ppermute | solution.py:28
  385.0 7.5 %collective-permute-start.33 = (bf16[56,576]{1,0:T(8,128)(2,1)S(1)}, bf16[56,576]{1,0:T(8,128)(2,1)S(1)}, u32[]{:S(2)}, u32[]{:S(2)}) collective-permute-start(bf16[56,576]{1,0:T(8,128)(2,1)S(1)} %get-tuple-element.113), channel_id=1, source_target_pairs={{0,4},{1,5},{2,6},{3,7},{4,0},{5,1},{6,2},{7,3},{8,12},{9,13},{10,... | collective-permute-start | bytes 193544 | tf_op jit(solution)/shard_map/ppermute | solution.py:28
  385.1 7.5 %collective-permute-start.32 = (bf16[56,576]{1,0:T(8,128)(2,1)S(1)}, bf16[56,576]{1,0:T(8,128)(2,1)S(1)}, u32[]{:S(2)}, u32[]{:S(2)}) collective-permute-start(bf16[56,576]{1,0:T(8,128)(2,1)S(1)} %get-tuple-element.114), channel_id=1, source_target_pairs={{0,2},{1,3},{2,0},{3,1},{4,6},{5,7},{6,4},{7,5},{8,10},{9,11},{10,... | collective-permute-start | bytes 193544 | tf_op jit(solution)/shard_map/ppermute | solution.py:28
  394.6 10.1 %collective-permute-start.37 = (bf16[384,768]{1,0:T(8,128)(2,1)}, bf16[384,768]{1,0:T(8,128)(2,1)S(1)}, u32[]{:S(2)}, u32[]{:S(2)}) collective-permute-start(bf16[384,768]{1,0:T(8,128)(2,1)} %bitcast.408), channel_id=1, source_target_pairs={{0,16},{16,0},{1,17},{17,1},{2,18},{18,2},{3,19},{19,3},{4,20},{20... | collective-permute-start | bytes 1769480 | tf_op jit(solution)/shard_map/ppermute | solution.py:28
  406.1 1.8 collective-permute-start.38
  (44 other events, 214.8 us)
Sparse Core Ops, SparseCore 0:
  22.2 76.4 all-gather.2
  256.5 106.3 reduce-scatter.1
